TPU v7x, 256 devices: a whole 4x4x8 slice. The times are simulated.
256 devices in a mesh: row: 32 (over x, y, core), col: 8 (over z).
Axes of the slice: x: 4, y: 4, z: 8, core: 2. Of those that a mesh axis runs over, the one named last changes fastest.
Arguments:
- features: bfloat16 [65536, 256], P(('row', 'col')), may hold values from -6 to 6
- weight: bfloat16 [256, 256], replicated, may hold values from -0.375 to 0.375
- tile_values: bfloat16 [24576, 128, 128], P(('row', 'col')), may hold values from -0.21582031 to 0.21582031
- tile_coords: int32 [24576, 2], P(('row', 'col')), may hold values from 0 to 63, as said below
- tile_count: int32 [256], P(('row', 'col')), may hold values from 1 to 96, as said below
- cotangent: bfloat16 [65536, 256], P(('row', 'col')), may hold values from -6 to 6
Outputs:
- hidden: bfloat16 [65536, 256], P(('row', 'col'))
- weight_grad: float32 [256, 256], P('row')
- feature_grad: float32 [65536, 256], P(('row', 'col'))
Inputs may be any that keep to these rules, and one draw needn't show every extreme that they name: Device d = a 8 + b uses its first tile_count[d] slots; some device uses all 96. `tile_coords`: column 0 is a local row tile below 16, column 1 a local column tile below 64. A device's 96 slots name distinct (row tile, column tile) positions.
All inputs are finite; a program needn't handle non-finite values.
Results may differ from a plain program's by a relative error of at most 0.006.
Values may be sent and summed in bfloat16 or wider, within the bound.
A program may use at most 128 MiB of HBM per device.

v0:
```python
import jax
import jax.numpy as jnp
from jax import lax
from jax.sharding import PartitionSpec as P

gelu_scale = 0.7978845608028654
gelu_cubic = 0.044715


def gelu_pair(values):
    inner = gelu_scale * (values + gelu_cubic * values * values * values)
    slope_tanh = jnp.tanh(inner)
    result = 0.5 * values * (1.0 + slope_tanh)
    slope = 0.5 * (1.0 + slope_tanh) + 0.5 * values * (
        1.0 - slope_tanh * slope_tanh
    ) * gelu_scale * (1.0 + 3.0 * gelu_cubic * values * values)
    return (result, slope)


def tile_sums(first_tile, count_tiles, ids, live, products):
    local_ids = ids - first_tile
    inside = live & (local_ids >= 0) & (local_ids < count_tiles)
    target = jnp.where(inside, local_ids, count_tiles)
    empty = jnp.zeros((count_tiles,) + products.shape[1:], jnp.float32)
    return empty.at[target].add(products, mode="drop")


def per_device(features, weight, tile_values, tile_coords, tile_count, cotangent):
    tile_size = tile_values.shape[1]
    width = features.shape[1]
    slots = tile_values.shape[0]
    own_rows = features.shape[0]
    live = jnp.arange(slots) < tile_count[0]
    row_ids = tile_coords[:, 0]
    col_ids = tile_coords[:, 1]
    panels = lax.all_gather(features, "row", axis=0, tiled=True)
    col_tiles = panels.shape[0] // tile_size
    row_tiles = lax.axis_size("col") * own_rows // tile_size
    picked = panels.reshape(col_tiles, tile_size, width)[col_ids]
    products = jnp.einsum("kab,kbf->kaf", tile_values, picked, preferred_element_type=jnp.float32)
    partial_value = tile_sums(0, row_tiles, row_ids, live, products).reshape(
        row_tiles * tile_size, width
    )
    aggregated = lax.psum_scatter(partial_value, "col", scatter_dimension=0, tiled=True)
    agg_rows = aggregated.astype(jnp.bfloat16)
    pre = jnp.dot(agg_rows, weight, preferred_element_type=jnp.float32)
    result, slope = gelu_pair(pre)
    hidden = result.astype(jnp.bfloat16)
    grad_pre = (cotangent.astype(jnp.float32) * slope).astype(jnp.bfloat16)
    partial_weight = lax.dot_general(
        agg_rows, grad_pre, (((0,), (0,)), ((), ())), preferred_element_type=jnp.float32
    )
    total_weight = lax.psum(partial_weight, ("row", "col"))
    share = width // lax.axis_size("row")
    weight_grad = lax.dynamic_slice_in_dim(total_weight, lax.axis_index("row") * share, share, 0)
    grad_agg = lax.dot_general(
        grad_pre, weight, (((1,), (1,)), ((), ())), preferred_element_type=jnp.float32
    ).astype(jnp.bfloat16)
    block_grad = lax.all_gather(grad_agg, "col", axis=0, tiled=True)
    chosen = block_grad.reshape(row_tiles, tile_size, width)[row_ids]
    backward = jnp.einsum("kba,kbf->kaf", tile_values, chosen, preferred_element_type=jnp.float32)
    summed = tile_sums(0, col_tiles, col_ids, live, backward).reshape(col_tiles * tile_size, width)
    feature_grad = lax.psum_scatter(summed, "row", scatter_dimension=0, tiled=True)
    return (hidden, weight_grad, feature_grad)


def solution(mesh):
    return jax.shard_map(
        per_device,
        mesh=mesh,
        in_specs=(
            P(("row", "col"), None),
            P(),
            P(("row", "col"), None, None),
            P(("row", "col"), None),
            P(("row", "col")),
            P(("row", "col"), None),
        ),
        out_specs=(P(("row", "col"), None), P("row", None), P(("row", "col"), None)),
        check_vma=False,
    )
```

profile of v0, /device:TPU:1, one launch (start us, length us, event | category | flops | bytes accessed | tf_op | source)
XLA Modules:
  0.0 569.3 jit_solution(13865863993692188379)
XLA Ops:
  7.2 0.0 copy-start
  7.2 0.0 all-gather.3.cloned.1.call-start
  7.2 0.7 all-gather.3.cloned.1.call-update
  7.9 0.0 reduce-scatter.3.cloned.1.call-start
  8.8 0.8 fusion.14
  9.6 56.4 %all-gather.3.cloned.1.call-done = bf16[8192,256]{1,0:T(8,128)(2,1)} async-done(((bf16[256,256]{1,0:T(8,128)(2,1)}), bf16[8192,256]{1,0:T(8,128)(2,1)}) %all-gather.3.cloned.1.call-update) | async-done | bytes 4194320 | tf_op jit(solution)/shard_map/all_gather | solution.py:36
  65.9 8.2 %gather_fusion = bf16[96,128,256]{2,1,0:T(8,128)(2,1)} fusion(bf16[64,128,256]{2,1,0:T(8,128)(2,1)} %bitcast.29, s32[1024]{0:T(1024)S(1)} %pad_clamp_fusion.1), kind=kCustom, calls=%fused_computation | custom fusion | bytes 12583296 | tf_op jit(solution)/shard_map/gather | solution.py:39
  74.1 9.1 %convolution_bitcast_fusion.1 = f32[96,128,256]{1,2,0:T(8,128)} fusion(bf16[96,128,256]{2,1,0:T(8,128)(2,1)} %gather_fusion, bf16[96,128,128]{2,1,0:T(8,128)(2,1)S(1)} %copy-done), kind=kOutput, calls=%fused_computation.5 | convolution fusion | flops 805306368 | bytes 22020096 | tf_op jit(solution)/shard_map/kab,kbf->kaf/dot_general | solution.py:40
  83.2 12.6 %copy.12 = f32[96,128,256]{2,1,0:T(8,128)} copy(f32[96,128,256]{1,2,0:T(8,128)} %convolution_bitcast_fusion.1) | data formatting | bytes 25165824 | tf_op jit(solution)/shard_map/kab,kbf->kaf/dot_general | solution.py:40
  95.8 1.6 broadcast_in_dim.7
  97.4 25.8 %scatter_fusion = f32[16,128,256]{2,1,0:T(8,128)} fusion(f32[16,128,256]{2,1,0:T(8,128)} %broadcast_in_dim.7, s32[96]{0:T(128)S(1)} %get-tuple-element.6, f32[96,128,256]{2,1,0:T(8,128)} %copy.12), kind=kCustom, calls=%fused_computation.2 | custom fusion | flops 3145728 | bytes 37749120 | tf_op jit(solution)/shard_map/scatter-add | solution.py:25
  123.2 0.0 reduce-scatter.3.cloned.1.call-update
  123.2 0.0 all-gather.5.cloned.1.call-start
  123.2 38.8 %reduce-scatter.3.cloned.1.call-done = f32[256,256]{1,0:T(8,128)} async-done(((f32[2048,256]{1,0:T(8,128)}), f32[256,256]{1,0:T(8,128)}) %reduce-scatter.3.cloned.1.call-update) | async-done | bytes 262160 | tf_op jit(solution)/shard_map/reduce_scatter | solution.py:44
  162.0 0.0 copy-done.3
  162.0 2.0 fusion.6
  163.9 0.9 convolution_convert_fusion
  164.8 0.0 all-gather.5.cloned.1.call-update
  164.9 0.0 all-reduce.2.cloned.1.call-start
  164.9 1.9 fusion.7
  166.8 0.0 all-reduce.2.cloned.1.call-update
  166.8 0.2 reduce-scatter.5.cloned.1.call-start
  167.1 34.9 %all-gather.5.cloned.1.call-done = bf16[2048,256]{1,0:T(8,128)(2,1)} async-done(((bf16[256,256]{1,0:T(8,128)(2,1)}), bf16[2048,256]{1,0:T(8,128)(2,1)}) %all-gather.5.cloned.1.call-update) | async-done | bytes 1048592 | tf_op jit(solution)/shard_map/all_gather | solution.py:59
  202.0 7.2 %gather_fusion.1 = bf16[96,128,256]{2,1,0:T(8,128)(2,1)} fusion(bf16[16,128,256]{2,1,0:T(8,128)(2,1)} %bitcast.28, s32[1024]{0:T(1024)S(1)} %pad_clamp_fusion), kind=kCustom, calls=%fused_computation.1 | custom fusion | bytes 12583296 | tf_op jit(solution)/shard_map/gather | solution.py:60
  209.2 9.1 %convolution_bitcast_fusion = f32[96,128,256]{1,2,0:T(8,128)} fusion(bf16[96,128,256]{2,1,0:T(8,128)(2,1)} %gather_fusion.1, bf16[96,128,128]{2,1,0:T(8,128)(2,1)S(1)} %copy-done), kind=kOutput, calls=%fused_computation.4 | convolution fusion | flops 805306368 | bytes 22020096 | tf_op jit(solution)/shard_map/kba,kbf->kaf/dot_general | solution.py:61
  218.3 12.6 %copy.14 = f32[96,128,256]{2,1,0:T(8,128)} copy(f32[96,128,256]{1,2,0:T(8,128)} %convolution_bitcast_fusion) | data formatting | bytes 25165824 | tf_op jit(solution)/shard_map/kba,kbf->kaf/dot_general | solution.py:61
  230.9 4.2 broadcast_in_dim.14
  235.1 26.0 %scatter_fusion.1 = f32[64,128,256]{2,1,0:T(8,128)} fusion(f32[64,128,256]{2,1,0:T(8,128)} %broadcast_in_dim.14, s32[96]{0:T(128)S(1)} %get-tuple-element.8, f32[96,128,256]{2,1,0:T(8,128)} %copy.14), kind=kCustom, calls=%fused_computation.3 | custom fusion | flops 3145728 | bytes 37749120 | tf_op jit(solution)/shard_map/scatter-add | solution.py:25
  261.1 0.0 reduce-scatter.5.cloned.1.call-update
  261.1 198.5 %all-reduce.2.cloned.1.call-done = f32[256,256]{1,0:T(8,128)} async-done(((f32[256,256]{1,0:T(8,128)}), f32[256,256]{1,0:T(8,128)}) %all-reduce.2.cloned.1.call-update) | async-done | bytes 262160 | tf_op jit(solution)/shard_map/psum | solution.py:53
  459.6 1.3 constant_dynamic-slice_fusion
  460.9 101.9 %reduce-scatter.5.cloned.1.call-done = f32[256,256]{1,0:T(8,128)} async-done(((f32[8192,256]{1,0:T(8,128)}), f32[256,256]{1,0:T(8,128)}) %reduce-scatter.5.cloned.1.call-update) | async-done | bytes 262160 | tf_op jit(solution)/shard_map/reduce_scatter | solution.py:63
  (8 shorter events, 0.0 us)
Async XLA Ops:
  7.2 67.0 %copy-start = (bf16[96,128,128]{2,1,0:T(8,128)(2,1)S(1)}, bf16[96,128,128]{2,1,0:T(8,128)(2,1)}, u32[]{:S(2)}) copy-start(bf16[96,128,128]{2,1,0:T(8,128)(2,1)} %param.8) | copy-start | bytes 9437188
  7.2 58.7 %all-gather.3.cloned.1.call-start = ((), (), s32[]{:S(2)}) async-start(), calls=%async_computation.2 | async-start | bytes 4325376 | tf_op jit(solution)/shard_map/all_gather | solution.py:36
  7.9 154.1 %reduce-scatter.3.cloned.1.call-start = ((), (), s32[]{:S(2)}) async-start(), calls=%async_computation.3 | async-start | bytes 2359296 | tf_op jit(solution)/shard_map/reduce_scatter | solution.py:44
  97.4 64.6 %copy-start.2 = (bf16[256,256]{1,0:T(8,128)(2,1)S(1)}, bf16[256,256]{1,0:T(8,128)(2,1)}, u32[]{:S(2)}) copy-start(bf16[256,256]{1,0:T(8,128)(2,1)} %param.7) | copy-start | bytes 393220
  97.4 64.6 %copy-start.3 = (bf16[256,256]{1,0:T(8,128)(2,1)S(1)}, bf16[256,256]{1,0:T(8,128)(2,1)}, u32[]{:S(2)}) copy-start(bf16[256,256]{1,0:T(8,128)(2,1)} %param.11) | copy-start | bytes 393220
  123.2 78.8 %all-gather.5.cloned.1.call-start = ((), (), s32[]{:S(2)}) async-start(), calls=%async_computation.5 | async-start | bytes 1179648 | tf_op jit(solution)/shard_map/all_gather | solution.py:59
  164.9 294.8 %all-reduce.2.cloned.1.call-start = ((), (), s32[]{:S(2)}) async-start(), calls=%async_computation.4 | async-start | bytes 524288 | tf_op jit(solution)/shard_map/psum | solution.py:53
  166.8 395.9 %reduce-scatter.5.cloned.1.call-start = ((), (), s32[]{:S(2)}) async-start(), calls=%async_computation.6 | async-start | bytes 8650752 | tf_op jit(solution)/shard_map/reduce_scatter | solution.py:63
  235.1 327.7 %copy-start.1 = (bf16[96,128,128]{2,1,0:T(8,128)(2,1)S(1)}, bf16[96,128,128]{2,1,0:T(8,128)(2,1)}, u32[]{:S(2)}) copy-start(bf16[96,128,128]{2,1,0:T(8,128)(2,1)} %param.8) | copy-start | bytes 9437188
Sparse Core Ops, SparseCore 0:
  10.6 55.2 all-gather.2
  123.3 38.6 reduce-scatter.2
  165.0 36.9 all-gather.4
  207.3 252.3 all-reduce.1
  464.1 98.6 reduce-scatter.4
where the time goes:
time: 570 us; the launch traced here: 569 us
  waiting for transfers between devices  431 us (76%)
  other arithmetic  52.6 us (9%)
  local copies, waits for them, and re-layouts  47.7 us (8%)
  matrix products  22.9 us (4%)
  between operations  14.6 us (3%)
    psum x1, waiting for transfers between devices, per_device(): total_weight = lax.psum(partial_weight, ('row', 'col'))  198 us
    reduce_scatter x1, waiting for transfers between devices, per_device(): lax.psum_scatter(summed, 'row', scatter_dimension=0, tiled=True)  102 us
    all_gather x1, waiting for transfers between devices, per_device(): panels = lax.all_gather(features, 'row', axis=0, tiled=True)  56.4 us
    scatter-add x2, other arithmetic, tile_sums(): return empty.at[target].add(products, mode='drop')  51.8 us
    reduce_scatter x1, waiting for transfers between devices, per_device(): lax.psum_scatter(partial_value, 'col', scatter_dimension=0, tiled=True)  38.8 us
    all_gather x1, waiting for transfers between devices, per_device(): block_grad = lax.all_gather(grad_agg, 'col', axis=0, tiled=True)  34.9 us
    dot_general x1, local copies, waits for them, and re-layouts, per_device(): jnp.einsum('kba,kbf->kaf', tile_values, chosen, preferred_element_type=jn...  12.6 us
    dot_general x1, local copies, waits for them, and re-layouts, per_device(): jnp.einsum('kab,kbf->kaf', tile_values, picked, preferred_element_type=jn...  12.6 us
  transfers between devices with their start and end apart: 5, of which 5 were waited for; matrix products, arithmetic and copies ran while one was open for 11% of the time, Pallas kernels for 0%

commit v1 on v0

v1 whole, which is shorter than its diff:
```python
import functools

import jax
import jax.numpy as jnp
from jax import lax
from jax.experimental import pallas as pl
from jax.experimental.pallas import tpu as pltpu
from jax.sharding import PartitionSpec as P

gelu_scale = 0.7978845608028654
gelu_cubic = 0.044715

MESH = pl.DeviceIdType.MESH
BF16 = jnp.bfloat16
F32 = jnp.float32
T = 128
HALF = 64
SIDE = 4
RING = 8
SLOTS = 96
ROW_TILES = 16
COL_TILES = 64
UNROLL = 4

PREV_F, LAST_F, PREV_B, LAST_B, ROW_ID, COL_ID = range(6)

OFFS = (0, -1, 1, 2)


def gelu_pair(values):
    inner = gelu_scale * (values + gelu_cubic * values * values * values)
    slope_tanh = jnp.tanh(inner)
    result = 0.5 * values * (1.0 + slope_tanh)
    slope = 0.5 * (1.0 + slope_tanh) + 0.5 * values * (
        1.0 - slope_tanh * slope_tanh
    ) * gelu_scale * (1.0 + 3.0 * gelu_cubic * values * values)
    return (result, slope)


def scratch():
    tile2 = (2, T, T)
    dma = pltpu.SemaphoreType.DMA
    return {
        "tiles": pltpu.VMEM((SLOTS, T, T), BF16),
        "weight_v": pltpu.VMEM((256, 256), BF16),
        "cot_v": pltpu.VMEM((256, 256), BF16),
        "coords_v": pltpu.VMEM((SLOTS, 2), jnp.int32),
        "table_v": pltpu.VMEM((8, T), jnp.int32),
        "table": pltpu.SMEM((8, T), jnp.int32),
        "panel0": pltpu.VMEM((COL_TILES, T, T), BF16),
        "panel1": pltpu.VMEM((COL_TILES, T, T), BF16),
        "sums0": pltpu.VMEM((SLOTS + 1, T, T), F32),
        "sums1": pltpu.VMEM((SLOTS + 1, T, T), F32),
        "zs": pltpu.VMEM((2, 2, 4) + tile2, BF16),
        "zr": pltpu.VMEM((2, 2, 4) + tile2, BF16),
        "agg": pltpu.VMEM((256, 256), BF16),
        "hid_v": pltpu.VMEM((256, 256), BF16),
        "wg": pltpu.VMEM((32, 8, 256), F32),
        "wg_row": pltpu.VMEM((32, 8, 256), F32),
        "wg_part": pltpu.VMEM((8, 256), F32),
        "wg_col": pltpu.VMEM((8, 8, 256), F32),
        "wg_out": pltpu.VMEM((8, 256), F32),
        "ga0": pltpu.VMEM((ROW_TILES, T, T), BF16),
        "ga1": pltpu.VMEM((ROW_TILES, T, T), BF16),
        "ps": pltpu.VMEM((2, 2, 4, 4, T, T), BF16),
        "pr": pltpu.VMEM((2, 2, 4, 4, T, T), BF16),
        "s1": pltpu.VMEM((2, 2, 4, T, T), BF16),
        "r1": pltpu.VMEM((2, 2, 2, 4, HALF, T), BF16),
        "s2": pltpu.VMEM((2, 2, 2, 4, T, T), BF16),
        "r2": pltpu.VMEM((2, 2, 2, 4, T, T), BF16),
        "axis_sum": pltpu.VMEM((2, 2, 4, T, T), F32),
        "s3": pltpu.VMEM((2, 2, T, T), BF16),
        "r3": pltpu.VMEM((2, 2, 2, HALF, T), BF16),
        "s4": pltpu.VMEM((2, 2, 2, T, T), BF16),
        "r4": pltpu.VMEM((2, 2, 2, T, T), BF16),
        "fg_v": pltpu.VMEM((256, 256), F32),
        "local_sem": dma((12,)),
        "send_sem": dma((240,)),
        "a_sem": dma((2, 2, 20)),
        "ap_sem": dma((2, 2, 16)),
        "z_sem": dma((2, 2, 4)),
        "d_sem": dma((2, 2, 4)),
        "p_sem": dma((2, 2, 4)),
        "r1_sem": dma((2, 2, 2)),
        "r2_sem": dma((2, 2, 2)),
        "r3_sem": dma((2, 2, 2)),
        "r4_sem": dma((2, 2, 2)),
        "wr_send": dma((32,)),
        "wr_recv": dma((32,)),
        "wc_send": dma((8,)),
        "wc_recv": dma((8,)),
    }


class Layer:
    def __init__(self, count, features, weight, tile_values, coords, cotangent, hidden, weight_grad, feature_grad, refs):
        self.__dict__.update(refs)
        self.count = count
        self.features, self.weight, self.tile_values = features, weight, tile_values
        self.coords, self.cotangent = coords, cotangent
        self.hidden, self.weight_grad, self.feature_grad = hidden, weight_grad, feature_grad
        self.panel = (self.panel0, self.panel1)
        self.sums = (self.sums0, self.sums1)
        self.ga = (self.ga0, self.ga1)
        self.row = lax.axis_index("row")
        self.z = lax.axis_index("col")
        self.core = lax.rem(self.row, 2)
        self.at = (self.row // 8, lax.rem(self.row // 2, SIDE))
        self.sends = []

    def along(self, axis, step):
        return lax.rem(self.at[axis] + step % SIDE, SIDE)

    def row_of(self, x, y, core):
        return (x * SIDE + y) * 2 + core

    def neighbour(self, axis, step):
        spot = [self.at[0], self.at[1]]
        spot[axis] = self.along(axis, step)
        return (self.row_of(spot[0], spot[1], self.core), self.z)

    def partner(self):
        return (self.row_of(self.at[0], self.at[1], 1 - self.core), self.z)

    def ring(self, step):
        return lax.rem(self.z + step % RING, RING)

    def tile_at(self, piece, first, second, core):
        x, y = (first, second) if piece == 0 else (second, first)
        return self.row_of(x, y, core) * 2 + piece

    def near_tile(self, piece, step1, step2, core):
        first, second = piece, 1 - piece
        return self.tile_at(piece, self.along(first, step1), self.along(second, step2), core)

    def send(self, src, dst, sem, device):
        copy = pltpu.make_async_remote_copy(
            src_ref=src, dst_ref=dst, send_sem=self.send_sem.at[len(self.sends)],
            recv_sem=sem, device_id=device, device_id_type=MESH,
        )
        copy.start()
        self.sends.append(copy)

    def arrive(self, dst, sem):
        pltpu.make_async_remote_copy(
            src_ref=dst, dst_ref=dst, send_sem=self.send_sem.at[0],
            recv_sem=sem, device_id=self.partner(), device_id_type=MESH,
        ).wait_recv()

    def load(self):
        sem = self.local_sem
        half = [
            pltpu.make_async_copy(
                self.features.at[:, :, pl.ds(h * T, T)],
                self.panel[h].at[pl.ds(self.row * 2, 2)], sem.at[h])
            for h in range(2)
        ]
        coords = pltpu.make_async_copy(self.coords, self.coords_v, sem.at[2])
        tiles = pltpu.make_async_copy(self.tile_values, self.tiles, sem.at[3])
        weight = pltpu.make_async_copy(self.weight, self.weight_v, sem.at[4])
        cot = pltpu.make_async_copy(self.cotangent, self.cot_v, sem.at[5])
        for copy in (*half, coords, tiles, weight, cot):
            copy.start()
        self.own, self.coords_in, self.tiles_in, self.dense_in = half, coords, tiles, (weight, cot)

    def neighbours(self):
        return [
            self.partner(), self.neighbour(0, 1), self.neighbour(0, -1), self.neighbour(1, 1),
            self.neighbour(1, -1), (self.row, self.ring(1)), (self.row, self.ring(-1)),
        ]

    def greet(self):
        barrier = pltpu.get_barrier_semaphore()
        for device in self.neighbours():
            pl.semaphore_signal(barrier, inc=1, device_id=device, device_id_type=MESH)

    def met(self):
        pl.semaphore_wait(pltpu.get_barrier_semaphore(), 7)

    def index_table(self):
        self.coords_in.wait()
        slot = lax.broadcasted_iota(jnp.int32, (SLOTS, T), 0)
        lane = lax.broadcasted_iota(jnp.int32, (SLOTS, T), 1)
        live = slot < self.count[0]
        lines = [None] * 8
        for column, prev, last, ids in ((0, PREV_F, LAST_F, ROW_ID), (1, PREV_B, LAST_B, COL_ID)):
            down = jnp.broadcast_to(self.coords_v[:, column:column + 1], (SLOTS, T))
            across = jnp.sum(jnp.where(slot == lane, down, 0), axis=0, keepdims=True)
            earlier = live & (slot < lane) & (down == across)
            lines[prev] = jnp.max(jnp.where(earlier, slot + 1, 0), axis=0, keepdims=True)
            lines[last] = jnp.max(jnp.where(live & (down == lane), slot + 1, 0), axis=0, keepdims=True)
            lines[ids] = across
        for at, line in enumerate(lines):
            self.table_v[at:at + 1, :] = jnp.zeros((1, T), jnp.int32) if line is None else line
        copy = pltpu.make_async_copy(self.table_v, self.table, self.local_sem.at[6])
        copy.start()
        for h in range(2):
            self.sums[h][0] = jnp.zeros((T, T), F32)
        copy.wait()

    def gather_tile(self, h, piece, i, j):
        tile = self.panel[h].at[self.near_tile(piece, OFFS[i], OFFS[j], self.core)]
        self.send(tile, tile, self.ap_sem.at[h, piece, i * 4 + j], self.partner())

    def gather_across(self, h, piece, i):
        tile = self.panel[h].at[self.near_tile(piece, OFFS[i], 0, self.core)]
        self.send(tile, tile, self.a_sem.at[h, piece, 4 + 4 * i], self.neighbour(1 - piece, 1))
        self.send(tile, tile, self.a_sem.at[h, piece, 5 + 4 * i], self.neighbour(1 - piece, -1))

    def gather_own(self, h):
        self.own[h].wait()
        for piece in range(2):
            tile = self.panel[h].at[self.near_tile(piece, 0, 0, self.core)]
            self.send(tile, tile, self.a_sem.at[h, piece, 0], self.neighbour(piece, 1))
            self.send(tile, tile, self.a_sem.at[h, piece, 1], self.neighbour(piece, -1))
        for piece in range(2):
            self.gather_across(h, piece, 0)
        for piece in range(2):
            self.gather_tile(h, piece, 0, 0)

    def gather_first(self, h):
        for i, rows, onward in ((1, 0, 1), (2, HALF, -1)):
            for piece in range(2):
                at = self.near_tile(piece, OFFS[i], 0, self.core)
                self.arrive(self.panel[h].at[at], self.a_sem.at[h, piece, i - 1])
                part = self.panel[h].at[at, pl.ds(rows, HALF)]
                self.send(part, part, self.a_sem.at[h, piece, i + 1], self.neighbour(piece, onward))
                self.gather_across(h, piece, i)
                self.gather_tile(h, piece, i, 0)

    def gather_second(self, h):
        for piece in range(2):
            at = self.near_tile(piece, 2, 0, self.core)
            self.arrive(self.panel[h].at[at, pl.ds(0, HALF)], self.a_sem.at[h, piece, 2])
            self.arrive(self.panel[h].at[at, pl.ds(HALF, HALF)], self.a_sem.at[h, piece, 3])
            self.gather_across(h, piece, 3)
            self.gather_tile(h, piece, 3, 0)

    def gather_third(self, h, which=(0, 1, 2, 3)):
        for i in which:
            for j, rows, onward in ((1, 0, 1), (2, HALF, -1)):
                for piece in range(2):
                    at = self.near_tile(piece, OFFS[i], OFFS[j], self.core)
                    self.arrive(self.panel[h].at[at], self.a_sem.at[h, piece, 4 + 4 * i + j - 1])
                    part = self.panel[h].at[at, pl.ds(rows, HALF)]
                    self.send(part, part, self.a_sem.at[h, piece, 4 + 4 * i + j + 1], self.neighbour(1 - piece, onward))
                    self.gather_tile(h, piece, i, j)

    def gather_fourth(self, h):
        for i in range(4):
            for piece in range(2):
                at = self.near_tile(piece, OFFS[i], 2, self.core)
                self.arrive(self.panel[h].at[at, pl.ds(0, HALF)], self.a_sem.at[h, piece, 4 + 4 * i + 2])
                self.arrive(self.panel[h].at[at, pl.ds(HALF, HALF)], self.a_sem.at[h, piece, 4 + 4 * i + 3])
                self.gather_tile(h, piece, i, 3)

    def gather_partner(self, h):
        for i in range(4):
            for j in range(4):
                for piece in range(2):
                    at = self.near_tile(piece, OFFS[i], OFFS[j], 1 - self.core)
                    self.arrive(self.panel[h].at[at], self.ap_sem.at[h, piece, i * 4 + j])

    def slots(self, h, prev, ids, source, dims):
        sums = self.sums[h]

        def block(at, carry):
            for u in range(UNROLL):
                k = at * UNROLL + u
                product = lax.dot_general(
                    self.tiles[k], source[self.table[ids, k]], (dims, ((), ())), preferred_element_type=F32)
                sums[k + 1] = sums[self.table[prev, k]] + product
            return carry

        lax.fori_loop(0, SLOTS // UNROLL, block, 0)

    def forward(self, h):
        self.slots(h, PREV_F, COL_ID, self.panel[h], ((1,), (0,)))

    def backward(self, h):
        self.slots(h, PREV_B, ROW_ID, self.ga[h], ((0,), (0,)))

    def row_sum(self, h, tile):
        return self.sums[h][self.table[LAST_F, tile]]

    def col_sum(self, h, tile):
        return self.sums[h][self.table[LAST_B, tile]]

    def reduce_step(self, h, step):
        for way in range(2):
            sign = 1 - 2 * way
            block = self.ring(sign * (4 - step))
            stage = self.zs.at[h, way, step]
            if step == 0:
                stage[way] = self.row_sum(h, block * 2 + way).astype(BF16)
                self.send(stage.at[way], self.zr.at[h, way, step, way], self.z_sem.at[h, way, step], (self.row, self.ring(sign)))
                continue
            got = self.zr.at[h, way, step - 1]
            self.arrive(got.at[way] if step == 1 else got, self.z_sem.at[h, way, step - 1])
            for piece in range(2):
                value = self.row_sum(h, block * 2 + piece)
                if step > 1 or piece == way:
                    value = value + got[piece].astype(F32)
                stage[piece] = value.astype(BF16)
            self.send(stage, self.zr.at[h, way, step], self.z_sem.at[h, way, step], (self.row, self.ring(sign)))

    def reduce_end(self, h):
        for way in range(2):
            self.arrive(self.zr.at[h, way, 3], self.z_sem.at[h, way, 3])
        for piece in range(2):
            value = self.row_sum(h, self.z * 2 + piece)
            value = value + self.zr[h, 0, 3, piece].astype(F32) + self.zr[h, 1, 3, piece].astype(F32)
            self.agg[pl.ds(piece * T, T), pl.ds(h * T, T)] = value.astype(BF16)

    def dense(self):
        for copy in self.dense_in:
            copy.wait()
        pre = jnp.dot(self.agg[...], self.weight_v[...], preferred_element_type=F32)
        result, slope = gelu_pair(pre)
        grad_pre = (self.cot_v[...].astype(F32) * slope).astype(BF16)
        self.hid_v[...] = result.astype(BF16)
        grad_agg = lax.dot_general(
            grad_pre, self.weight_v[...], (((1,), (1,)), ((), ())), preferred_element_type=F32).astype(BF16)
        for h in range(2):
            for piece in range(2):
                self.ga[h][self.z * 2 + piece] = grad_agg[piece * T:(piece + 1) * T, h * T:(h + 1) * T]
        self.spread_own(0)
        self.spread_own(1)
        total = lax.dot_general(
            self.agg[...], grad_pre, (((0,), (0,)), ((), ())), preferred_element_type=F32)
        self.wg[...] = total.reshape(32, 8, 256)
        self.hidden_out = pltpu.make_async_copy(self.hid_v, self.hidden, self.local_sem.at[7])
        self.hidden_out.start()

    def weight_copy(self, step):
        there = lax.rem(self.row + step, 32)
        return pltpu.make_async_remote_copy(
            src_ref=self.wg.at[there], dst_ref=self.wg_row.at[self.row], send_sem=self.wr_send.at[step],
            recv_sem=self.wr_recv.at[step], device_id=(there, self.z), device_id_type=MESH)

    def weight_start(self):
        def start(step, carry):
            self.weight_copy(step).start()
            return carry

        lax.fori_loop(1, 32, start, 0)

    def weight_column_copy(self, step):
        there = lax.rem(self.z + step, RING)
        return pltpu.make_async_remote_copy(
            src_ref=self.wg_part, dst_ref=self.wg_col.at[self.z], send_sem=self.wc_send.at[step],
            recv_sem=self.wc_recv.at[step], device_id=(self.row, there), device_id_type=MESH)

    def weight_middle(self):
        def wait(step, carry):
            came = lax.rem(self.row + 32 - step, 32)
            pltpu.make_async_remote_copy(
                src_ref=self.wg.at[came], dst_ref=self.wg_row.at[came], send_sem=self.wr_send.at[step],
                recv_sem=self.wr_recv.at[step], device_id=(came, self.z), device_id_type=MESH).wait_recv()
            return carry

        lax.fori_loop(1, 32, wait, 0)
        self.wg_row[self.row] = self.wg[self.row]
        part = jnp.sum(self.wg_row[...], axis=0)
        self.wg_part[...] = part
        self.wg_col[self.z] = part

        def start(step, carry):
            self.weight_column_copy(step).start()
            return carry

        lax.fori_loop(1, RING, start, 0)

    def weight_end(self):
        def wait(step, carry):
            came = lax.rem(self.z + RING - step, RING)
            pltpu.make_async_remote_copy(
                src_ref=self.wg_part, dst_ref=self.wg_col.at[came], send_sem=self.wc_send.at[step],
                recv_sem=self.wc_recv.at[step], device_id=(self.row, came), device_id_type=MESH).wait_recv()
            return carry

        lax.fori_loop(1, RING, wait, 0)
        self.wg_out[...] = jnp.sum(self.wg_col[...], axis=0)
        out = pltpu.make_async_copy(self.wg_out, self.weight_grad, self.local_sem.at[8])
        out.start()
        return out

    def spread_own(self, h):
        mine = self.ga[h].at[pl.ds(self.z * 2, 2)]
        for way in range(2):
            self.send(mine, mine, self.d_sem.at[h, way, 0], (self.row, self.ring(1 - 2 * way)))

    def spread_step(self, h, step):
        for way in range(2):
            sign = 1 - 2 * way
            first = self.ring(-sign * step) * 2
            if step == 4:
                self.arrive(self.ga[h].at[first + way], self.d_sem.at[h, way, 3])
                continue
            block = self.ga[h].at[pl.ds(first, 2)]
            self.arrive(block, self.d_sem.at[h, way, step - 1])
            onward = self.ga[h].at[first + way] if step == 3 else block
            self.send(onward, onward, self.d_sem.at[h, way, step], (self.row, self.ring(sign)))

    def grad_tile(self, h, piece, keep, step, core):
        return self.col_sum(h, self.tile_at(piece, keep, self.along(1 - piece, step), core))

    def grad_partner(self, h):
        for at, step in enumerate((2, 1, -1, 0)):
            for piece in range(2):
                for keep in range(SIDE):
                    self.ps[h, piece, at, keep] = self.grad_tile(h, piece, keep, step, 1 - self.core).astype(BF16)
                self.send(self.ps.at[h, piece, at], self.pr.at[h, piece, at], self.p_sem.at[h, piece, at], self.partner())

    def chip_tile(self, h, piece, at, keep):
        step = (2, 1, -1, 0)[at]
        return self.grad_tile(h, piece, keep, step, self.core) + self.pr[h, piece, at, keep].astype(F32)

    def grad_first(self, h):
        for piece in range(2):
            self.arrive(self.pr.at[h, piece, 0], self.p_sem.at[h, piece, 0])
            for keep in range(SIDE):
                self.s1[h, piece, keep] = self.chip_tile(h, piece, 0, keep).astype(BF16)
            for way in range(2):
                self.send(
                    self.s1.at[h, piece, :, pl.ds(way * HALF, HALF)], self.r1.at[h, piece, way],
                    self.r1_sem.at[h, piece, way], self.neighbour(1 - piece, 1 - 2 * way))

    def grad_second(self, h):
        for piece in range(2):
            for way in range(2):
                self.arrive(self.pr.at[h, piece, 1 + way], self.p_sem.at[h, piece, 1 + way])
                self.arrive(self.r1.at[h, piece, way], self.r1_sem.at[h, piece, way])
                for keep in range(SIDE):
                    value = self.chip_tile(h, piece, 1 + way, keep)
                    added = value[way * HALF:(way + 1) * HALF] + self.r1[h, piece, way, keep].astype(F32)
                    plain = value[(1 - way) * HALF:(2 - way) * HALF]
                    self.s2[h, piece, way, keep, pl.ds(way * HALF, HALF)] = added.astype(BF16)
                    self.s2[h, piece, way, keep, pl.ds((1 - way) * HALF, HALF)] = plain.astype(BF16)
                self.send(
                    self.s2.at[h, piece, way], self.r2.at[h, piece, way],
                    self.r2_sem.at[h, piece, way], self.neighbour(1 - piece, 1 - 2 * way))

    def grad_third(self, h):
        for piece in range(2):
            self.arrive(self.pr.at[h, piece, 3], self.p_sem.at[h, piece, 3])
            for way in range(2):
                self.arrive(self.r2.at[h, piece, way], self.r2_sem.at[h, piece, way])
            for keep in range(SIDE):
                value = self.chip_tile(h, piece, 3, keep)
                value = value + self.r2[h, piece, 0, keep].astype(F32) + self.r2[h, piece, 1, keep].astype(F32)
                self.axis_sum[h, piece, keep] = value
            self.s3[h, piece] = self.axis_sum[h, piece, self.along(piece, 2)].astype(BF16)
            for way in range(2):
                self.send(
                    self.s3.at[h, piece, pl.ds(way * HALF, HALF)], self.r3.at[h, piece, way],
                    self.r3_sem.at[h, piece, way], self.neighbour(piece, 1 - 2 * way))

    def grad_fourth(self, h):
        for piece in range(2):
            for way in range(2):
                sign = 1 - 2 * way
                self.arrive(self.r3.at[h, piece, way], self.r3_sem.at[h, piece, way])
                value = self.axis_sum[h, piece, self.along(piece, sign)]
                added = value[way * HALF:(way + 1) * HALF] + self.r3[h, piece, way].astype(F32)
                plain = value[(1 - way) * HALF:(2 - way) * HALF]
                self.s4[h, piece, way, pl.ds(way * HALF, HALF)] = added.astype(BF16)
                self.s4[h, piece, way, pl.ds((1 - way) * HALF, HALF)] = plain.astype(BF16)
                self.send(
                    self.s4.at[h, piece, way], self.r4.at[h, piece, way],
                    self.r4_sem.at[h, piece, way], self.neighbour(piece, sign))

    def grad_end(self, h):
        for piece in range(2):
            for way in range(2):
                self.arrive(self.r4.at[h, piece, way], self.r4_sem.at[h, piece, way])
            value = self.axis_sum[h, piece, self.at[piece]]
            value = value + self.r4[h, piece, 0].astype(F32) + self.r4[h, piece, 1].astype(F32)
            self.fg_v[pl.ds(piece * T, T), pl.ds(h * T, T)] = value

    def finish(self):
        out = pltpu.make_async_copy(self.fg_v, self.feature_grad, self.local_sem.at[9])
        out.start()
        weight_out = self.weight_end()
        self.hidden_out.wait()
        for copy in self.sends:
            copy.wait_send()

        def drain_row(step, carry):
            self.weight_copy(step).wait_send()
            return carry

        def drain_column(step, carry):
            self.weight_column_copy(step).wait_send()
            return carry

        lax.fori_loop(1, 32, drain_row, 0)
        lax.fori_loop(1, RING, drain_column, 0)
        weight_out.wait()
        out.wait()

    def run(self):
        self.greet()
        self.load()
        self.index_table()
        self.met()
        self.gather_own(0)
        self.gather_own(1)
        self.gather_first(0)
        self.gather_second(0)
        self.gather_first(1)
        self.gather_third(0)
        self.gather_second(1)
        self.gather_fourth(0)
        self.gather_partner(0)
        self.tiles_in.wait()
        self.forward(0)
        self.reduce_step(0, 0)
        self.gather_third(1)
        self.gather_fourth(1)
        self.reduce_step(0, 1)
        self.gather_partner(1)
        self.forward(1)
        self.reduce_step(1, 0)
        self.reduce_step(0, 2)
        self.reduce_step(1, 1)
        self.reduce_step(0, 3)
        self.reduce_step(1, 2)
        self.reduce_end(0)
        self.reduce_step(1, 3)
        self.reduce_end(1)
        self.dense()
        self.weight_start()
        self.spread_step(0, 1)
        self.spread_step(1, 1)
        self.spread_step(0, 2)
        self.spread_step(1, 2)
        self.spread_step(0, 3)
        self.spread_step(0, 4)
        self.spread_step(1, 3)
        self.backward(0)
        self.grad_partner(0)
        self.spread_step(1, 4)
        self.grad_first(0)
        self.backward(1)
        self.grad_partner(1)
        self.grad_second(0)
        self.grad_first(1)
        self.weight_middle()
        self.grad_third(0)
        self.grad_second(1)
        self.grad_fourth(0)
        self.grad_third(1)
        self.grad_end(0)
        self.grad_fourth(1)
        self.grad_end(1)
        self.finish()


def kernel(names, *refs):
    count, features, weight, tile_values, coords, cotangent, hidden, weight_grad, feature_grad = refs[:9]
    named = dict(zip(names, refs[9:]))
    Layer(count, features, weight, tile_values, coords, cotangent, hidden, weight_grad, feature_grad, named).run()


def per_device(features, weight, tile_values, tile_coords, tile_count, cotangent):
    buffers = scratch()
    anywhere = pl.BlockSpec(memory_space=pl.ANY)
    return pl.pallas_call(
        functools.partial(kernel, tuple(buffers)),
        out_shape=(
            jax.ShapeDtypeStruct((256, 256), BF16),
            jax.ShapeDtypeStruct((8, 256), F32),
            jax.ShapeDtypeStruct((256, 256), F32),
        ),
        in_specs=[pl.BlockSpec(memory_space=pltpu.SMEM)] + [anywhere] * 5,
        out_specs=(anywhere, anywhere, anywhere),
        scratch_shapes=list(buffers.values()),
        compiler_params=pltpu.CompilerParams(
            collective_id=0, has_side_effects=True, vmem_limit_bytes=60 * 1024 * 1024),
        name="graph_layer",
    )(tile_count, features.reshape(2, 128, 256), weight, tile_values, tile_coords, cotangent)


def solution(mesh):
    return jax.shard_map(
        per_device,
        mesh=mesh,
        in_specs=(
            P(("row", "col"), None),
            P(),
            P(("row", "col"), None, None),
            P(("row", "col"), None),
            P(("row", "col")),
            P(("row", "col"), None),
        ),
        out_specs=(P(("row", "col"), None), P("row", None), P(("row", "col"), None)),
        check_vma=False,
    )
```

time: 570 us -> 111 us (0.19)
  waiting for transfers between devices: 431 us -> 0 us
  Pallas kernels: 0 us -> 104 us
  other arithmetic: 52.6 us -> 0 us
  local copies, waits for them, and re-layouts: 47.7 us -> 5.93 us
  matrix products: 22.9 us -> 0 us
  between operations: 14.6 us -> 1.29 us
    psum x1 -> x0, waiting for transfers between devices: 198 us -> none  [per_device(): total_weight = lax.psum(partial_weight, ('row', 'col'))]
    reduce_scatter x2 -> x0, waiting for transfers between devices: 141 us -> none  [the longest x1 102 us: per_device(): lax.psum_scatter(summed, 'row', scatter_dimension=0, tiled=True)]
    pallas_call x0 -> x1, Pallas kernels: none -> 104 us  [per_device(): pl.pallas_call(functools.partial(kernel, tuple(buffers)), out_shape=(jax....]
    all_gather x2 -> x0, waiting for transfers between devices: 91.2 us -> none  [the longest x1 56.4 us: per_device(): panels = lax.all_gather(features, 'row', axis=0, tiled=True)]
    scatter-add x2 -> x0, other arithmetic: 51.8 us -> none  [tile_sums(): return empty.at[target].add(products, mode='drop')]
    dot_general x2 -> x0, local copies, waits for them, and re-layouts: 25.2 us -> none  [the longest x1 12.6 us: per_device(): jnp.einsum('kba,kbf->kaf', tile_values, chosen, preferred_element_type=jn...]
    dot_general x5 -> x0, matrix products: 22.9 us -> none  [the longest x1 9.1 us: per_device(): jnp.einsum('kab,kbf->kaf', tile_values, picked, preferred_element_type=jn...]
    gather x2 -> x0, local copies, waits for them, and re-layouts: 15.4 us -> none  [the longest x1 8.2 us: per_device(): picked = panels.reshape(col_tiles, tile_size, width)[col_ids]]
  transfers between devices with their start and end apart: 5 -> 0, of which waited for: 5 -> 0; matrix products, arithmetic and copies ran while one was open for 11% -> 0% of each run, Pallas kernels for 0% -> 0%
where the time goes in v1:
time: 111 us
  Pallas kernels  104 us (94%)
  local copies, waits for them, and re-layouts  5.93 us (5%)
  between operations  1.29 us (1%)
    pallas_call x1, Pallas kernels, per_device(): pl.pallas_call(functools.partial(kernel, tuple(buffers)), out_shape=(jax....  104 us
    unnamed x4, local copies, waits for them, and re-layouts  5.93 us

profile of v1, /device:TPU:1, one launch (start us, length us, event | category | flops | bytes accessed | tf_op | source)
XLA Modules:
  0.0 110.9 jit_solution(4511701581068271754)
XLA Ops:
  1.3 1.4 %copy.9.refs_4_ = s32[96,2]{1,0:T(8,128)} copy(s32[96,2]{0,1:T(2,128)} %param.9) | data formatting | bytes 1536 | tf_op args[3]
  2.7 103.7 %graph_layer.1 = (bf16[256,256]{1,0:T(8,128)(2,1)}, f32[8,256]{1,0:T(8,128)}, f32[256,256]{1,0:T(8,128)}) custom-call(s32[1]{0:T(128)S(6)} %copy.13.refs_0_, bf16[2,128,256]{2,1,0:T(8,128)(2,1)} %bitcast.1, bf16[256,256]{1,0:T(8,128)(2,1)} %refs_2_.1, bf16[96,128,128]{2,1,0:T(8,128)(2,1)} %refs_3_.1, s32[96,2]{1,0:T(8,128)} %copy.9.refs_4_, ...), custom_call_target="tpu_custom_call" | custom-call | tf_op jit(solution)/shard_map/graph_layer/pallas_call | solution.py:569
  106.3 1.6 %copy.14 = bf16[256,256]{1,0:T(8,128)(2,1)} copy(bf16[256,256]{1,0:T(8,128)(2,1)} %get-tuple-element.6) | data formatting | bytes 262144
  107.9 1.3 %copy.15 = f32[8,256]{1,0:T(8,128)} copy(f32[8,256]{1,0:T(8,128)} %get-tuple-element.7) | data formatting | bytes 16384
  109.2 1.7 %copy.16 = f32[256,256]{1,0:T(8,128)} copy(f32[256,256]{1,0:T(8,128)} %get-tuple-element.8) | data formatting | bytes 524288

commit v2 on v0

v2 whole, which is shorter than its diff:
```python
import functools

import jax
import jax.numpy as jnp
from jax import lax
from jax.experimental import pallas as pl
from jax.experimental.pallas import tpu as pltpu
from jax.sharding import PartitionSpec as P

gelu_scale = 0.7978845608028654
gelu_cubic = 0.044715

MESH = pl.DeviceIdType.MESH
BF16 = jnp.bfloat16
F32 = jnp.float32
T = 128
SIDE = 4
RING = 8
SLOTS = 96
ROW_TILES = 16
COL_TILES = 64
UNROLL = 16

PREV_F, LAST_F, PREV_B, LAST_B, ROW_ID, PANEL_ID = range(6)

OTHERS = (2, 1, -1)


def gelu_pair(values):
    inner = gelu_scale * (values + gelu_cubic * values * values * values)
    slope_tanh = jnp.tanh(inner)
    result = 0.5 * values * (1.0 + slope_tanh)
    slope = 0.5 * (1.0 + slope_tanh) + 0.5 * values * (
        1.0 - slope_tanh * slope_tanh
    ) * gelu_scale * (1.0 + 3.0 * gelu_cubic * values * values)
    return (result, slope)


def scratch():
    dma = pltpu.SemaphoreType.DMA
    return {
        "tiles": pltpu.VMEM((SLOTS, T, T), BF16),
        "weight_v": pltpu.VMEM((256, 256), BF16),
        "cot_v": pltpu.VMEM((256, 256), BF16),
        "coords_v": pltpu.VMEM((2, SLOTS), jnp.int32),
        "table_v": pltpu.VMEM((8, SLOTS), jnp.int32),
        "table": pltpu.SMEM((8, SLOTS), jnp.int32),
        "panel0": pltpu.VMEM((COL_TILES, T, T), BF16),
        "panel1": pltpu.VMEM((COL_TILES, T, T), BF16),
        "sums0": pltpu.VMEM((SLOTS + 1, T, T), F32),
        "sums1": pltpu.VMEM((SLOTS + 1, T, T), F32),
        "zs": pltpu.VMEM((2, 2, 2, 4, T, T), BF16),
        "zr": pltpu.VMEM((2, 2, 2, 4, T, T), BF16),
        "agg": pltpu.VMEM((256, 256), BF16),
        "grad_pre": pltpu.VMEM((256, 256), BF16),
        "hid_v": pltpu.VMEM((256, 256), BF16),
        "wg": pltpu.VMEM((32, 8, 256), F32),
        "wg_row": pltpu.VMEM((32, 8, 256), F32),
        "wg_part": pltpu.VMEM((8, 256), F32),
        "wg_col": pltpu.VMEM((8, 8, 256), F32),
        "wg_out": pltpu.VMEM((8, 256), F32),
        "ga0": pltpu.VMEM((ROW_TILES, T, T), BF16),
        "ga1": pltpu.VMEM((ROW_TILES, T, T), BF16),
        "ps": pltpu.VMEM((2, 4, 2, SIDE, T, T), BF16),
        "pr": pltpu.VMEM((2, 4, 2, SIDE, T, T), BF16),
        "s1": pltpu.VMEM((2, 2, 3, SIDE, T, T), BF16),
        "r1": pltpu.VMEM((2, 2, 3, SIDE, T, T), BF16),
        "axis_sum": pltpu.VMEM((2, 2, SIDE, T, T), F32),
        "s2": pltpu.VMEM((2, 2, 3, T, T), BF16),
        "r2": pltpu.VMEM((2, 2, 3, T, T), BF16),
        "fg_v": pltpu.VMEM((256, 256), F32),
        "own_sem": dma((2,)),
        "in_sem": dma((5,)),
        "out_sem": dma((3,)),
        "a_send": dma((2,)),
        "a1_sem": dma((2, 2, 3)),
        "a2_sem": dma((2, 2, 4)),
        "ap_sem": dma((2,)),
        "z_send": dma((1,)),
        "z_sem": dma((2, 2, 2, 4)),
        "d_send": dma((1,)),
        "d_sem": dma((2, 2, 2, 4)),
        "e_send": dma((2,)),
        "p_sem": dma((2, 4)),
        "r1_sem": dma((2, 2)),
        "r2_sem": dma((2, 2)),
        "w_sem": dma((4,)),
    }


class Layer:
    def __init__(self, operands, results, refs):
        self.__dict__.update(refs)
        self.count, self.features, self.weight, self.tile_values, self.coords, self.cotangent = operands
        self.hidden, self.weight_grad, self.feature_grad = results
        self.panel = (self.panel0, self.panel1)
        self.sums = (self.sums0, self.sums1)
        self.ga = (self.ga0, self.ga1)
        self.row = lax.axis_index("row")
        self.z = lax.axis_index("col")
        self.core = lax.rem(self.row, 2)
        self.at = (self.row // 8, lax.rem(self.row // 2, SIDE))

    def along(self, axis, step):
        return lax.rem(self.at[axis] + step % SIDE, SIDE)

    def neighbour(self, axis, step):
        spot = [self.at[0], self.at[1]]
        spot[axis] = self.along(axis, step)
        return ((spot[0] * SIDE + spot[1]) * 2 + self.core, self.z)

    def partner(self):
        return (self.row + 1 - 2 * self.core, self.z)

    def ring(self, step):
        return lax.rem(self.z + step % RING, RING)

    def ring_device(self, way):
        return (self.row, self.ring(1 - 2 * way))

    def panel_at(self, piece, first, second, core):
        return ((piece * 2 + core) * SIDE + first) * SIDE + second

    def send(self, src, dst, send_sem, recv_sem, device):
        pltpu.make_async_remote_copy(
            src_ref=src, dst_ref=dst, send_sem=send_sem, recv_sem=recv_sem,
            device_id=device, device_id_type=MESH,
        ).start()

    def landed(self, ref, sem):
        pltpu.make_async_copy(ref, ref, sem).wait()

    def load(self):
        self.own = []
        for h in range(2):
            for piece in range(2):
                at = self.panel_at(piece, self.at[piece], self.at[1 - piece], self.core)
                copy = pltpu.make_async_copy(
                    self.features.at[pl.ds(piece * T, T), pl.ds(h * T, T)], self.panel[h].at[at], self.own_sem.at[h])
                copy.start()
        sem = self.in_sem
        self.coords_in = pltpu.make_async_copy(self.coords, self.coords_v, sem.at[0])
        self.tiles_in = pltpu.make_async_copy(self.tile_values, self.tiles, sem.at[1])
        self.dense_in = (
            pltpu.make_async_copy(self.weight, self.weight_v, sem.at[2]),
            pltpu.make_async_copy(self.cotangent, self.cot_v, sem.at[3]),
        )
        for copy in (self.coords_in, self.tiles_in, *self.dense_in):
            copy.start()

    def greet(self):
        barrier = pltpu.get_barrier_semaphore()
        for device in self.friends():
            pl.semaphore_signal(barrier, inc=1, device_id=device, device_id_type=MESH)

    def friends(self):
        around = [self.neighbour(axis, step) for axis in range(2) for step in OTHERS]
        return [self.partner(), self.ring_device(0), self.ring_device(1)] + around

    def met(self):
        pl.semaphore_wait(pltpu.get_barrier_semaphore(), 9)

    def index_table(self):
        self.coords_in.wait()
        slot = lax.broadcasted_iota(jnp.int32, (SLOTS, SLOTS), 0)
        lane = lax.broadcasted_iota(jnp.int32, (SLOTS, SLOTS), 1)
        live = slot < self.count[0]
        lines = [None] * 8
        for column, prev, last in ((0, PREV_F, LAST_F), (1, PREV_B, LAST_B)):
            across = self.coords_v[column:column + 1, :]
            down = jnp.sum(jnp.where(slot == lane, across, 0), axis=1, keepdims=True)
            earlier = live & (slot < lane) & (down == across)
            lines[prev] = jnp.max(jnp.where(earlier, slot + 1, 0), axis=0, keepdims=True)
            lines[last] = jnp.max(jnp.where(live & (down == lane), slot + 1, 0), axis=0, keepdims=True)
            if column == 0:
                lines[ROW_ID] = across
            else:
                x, y, core, piece = across // 16, (across // 4) % 4, (across // 2) % 2, across % 2
                straight = piece == 0
                lines[PANEL_ID] = self.panel_at(piece, jnp.where(straight, x, y), jnp.where(straight, y, x), core)
        for at, line in enumerate(lines):
            self.table_v[at:at + 1, :] = jnp.zeros((1, SLOTS), jnp.int32) if line is None else line
        copy = pltpu.make_async_copy(self.table_v, self.table, self.in_sem.at[4])
        copy.start()
        for h in range(2):
            self.sums[h][0] = jnp.zeros((T, T), F32)
        copy.wait()

    def gather_across(self, h, piece, step1):
        first = self.along(piece, step1)
        at = self.panel_at(piece, first, self.at[1 - piece], self.core)
        tile = self.panel[h].at[at]
        for step in OTHERS:
            self.send(tile, tile, self.a_send.at[h], self.a2_sem.at[h, piece, step1 % SIDE], self.neighbour(1 - piece, step))

    def gather_own(self, h):
        self.landed(self.panel[h].at[pl.ds(0, 2)], self.own_sem.at[h])
        for piece in range(2):
            at = self.panel_at(piece, self.at[piece], self.at[1 - piece], self.core)
            tile = self.panel[h].at[at]
            for step in OTHERS:
                self.send(tile, tile, self.a_send.at[h], self.a1_sem.at[h, piece, step % SIDE - 1], self.neighbour(piece, step))
        for piece in range(2):
            self.gather_across(h, piece, 0)

    def gather_first(self, h):
        for step in (1, -1, 2):
            for piece in range(2):
                came = self.panel_at(piece, self.along(piece, -step), self.at[1 - piece], self.core)
                self.landed(self.panel[h].at[came], self.a1_sem.at[h, piece, step % SIDE - 1])
                self.gather_across(h, piece, -step)

    def gather_second(self, h):
        for step1 in (0, -1, 1, 2):
            for piece in range(2):
                first = self.panel_at(piece, self.along(piece, step1), 0, self.core)
                self.landed(self.panel[h].at[pl.ds(first, 3)], self.a2_sem.at[h, piece, step1 % SIDE])
                line = self.panel[h].at[pl.ds(first, SIDE)]
                self.send(line, line, self.a_send.at[h], self.ap_sem.at[h], self.partner())

    def gather_partner(self, h):
        self.landed(self.panel[h].at[pl.ds(0, 32)], self.ap_sem.at[h])

    def forward(self, h):
        sums, panel = self.sums[h], self.panel[h]

        def block(at, carry):
            for u in range(UNROLL):
                k = at * UNROLL + u
                product = jnp.dot(self.tiles[k], panel[self.table[PANEL_ID, k]], preferred_element_type=F32)
                sums[k + 1] = sums[self.table[PREV_F, k]] + product
            return carry

        lax.fori_loop(0, SLOTS // UNROLL, block, 0)

    def backward(self, h):
        sums, ga = self.sums[h], self.ga[h]

        def block(at, carry):
            for u in range(UNROLL):
                k = at * UNROLL + u
                product = jnp.dot(ga[self.table[ROW_ID, k]], self.tiles[k], preferred_element_type=F32)
                sums[k + 1] = sums[self.table[PREV_B, k]] + product
            return carry

        lax.fori_loop(0, SLOTS // UNROLL, block, 0)

    def reduce_step(self, h, piece, step):
        for way in range(2):
            if step == 0 and way != piece:
                continue
            sign = 1 - 2 * way
            block = self.ring(sign * (4 - step))
            value = self.sums[h][self.table[LAST_F, block * 2 + piece]]
            if step > 1 or (step == 1 and way == piece):
                self.landed(self.zr.at[h, piece, way, step - 1], self.z_sem.at[h, piece, way, step - 1])
                value = value + self.zr[h, piece, way, step - 1].astype(F32)
            self.zs[h, piece, way, step] = value.astype(BF16)
            self.send(
                self.zs.at[h, piece, way, step], self.zr.at[h, piece, way, step], self.z_send.at[0],
                self.z_sem.at[h, piece, way, step], self.ring_device(way))

    def reduce_end(self, h, piece):
        value = self.sums[h][self.table[LAST_F, self.z * 2 + piece]]
        for way in range(2):
            self.landed(self.zr.at[h, piece, way, 3], self.z_sem.at[h, piece, way, 3])
            value = value + self.zr[h, piece, way, 3].astype(F32)
        self.agg[piece * T:(piece + 1) * T, h * T:(h + 1) * T] = value.astype(BF16)

    def dense(self, piece):
        rows = slice(piece * T, (piece + 1) * T)
        if piece == 0:
            for copy in self.dense_in:
                copy.wait()
        pre = jnp.dot(self.agg[rows, :], self.weight_v[...], preferred_element_type=F32)
        result, slope = gelu_pair(pre)
        grad_pre = (self.cot_v[rows, :].astype(F32) * slope).astype(BF16)
        turned = lax.dot_general(
            self.weight_v[...], grad_pre, (((1,), (1,)), ((), ())), preferred_element_type=F32).astype(BF16)
        for h in range(2):
            self.ga[h][self.z * 2 + piece] = turned[h * T:(h + 1) * T]
        self.hid_v[rows, :] = result.astype(BF16)
        self.grad_pre[rows, :] = grad_pre
        for h in range(2):
            mine = self.ga[h].at[self.z * 2 + piece]
            for way in range(2):
                self.send(mine, mine, self.d_send.at[0], self.d_sem.at[h, piece, way, 0], self.ring_device(way))

    def weight_start(self):
        self.hidden_out = pltpu.make_async_copy(self.hid_v, self.hidden, self.out_sem.at[0])
        self.hidden_out.start()
        total = lax.dot_general(
            self.agg[...], self.grad_pre[...], (((0,), (0,)), ((), ())), preferred_element_type=F32)
        self.wg[...] = total.reshape(32, 8, 256)

        def start(step, carry):
            there = lax.rem(self.row + step, 32)
            self.send(self.wg.at[there], self.wg_row.at[self.row], self.w_sem.at[0], self.w_sem.at[1], (there, self.z))
            return carry

        lax.fori_loop(1, 32, start, 0)

    def weight_middle(self):
        self.landed(self.wg_row.at[pl.ds(0, 31)], self.w_sem.at[1])
        self.wg_row[self.row] = self.wg[self.row]
        part = jnp.sum(self.wg_row[...], axis=0)
        self.wg_part[...] = part
        self.wg_col[self.z] = part

        def start(step, carry):
            there = lax.rem(self.z + step, RING)
            self.send(self.wg_part, self.wg_col.at[self.z], self.w_sem.at[2], self.w_sem.at[3], (self.row, there))
            return carry

        lax.fori_loop(1, RING, start, 0)

    def weight_end(self):
        self.landed(self.wg_col.at[pl.ds(0, 7)], self.w_sem.at[3])
        self.wg_out[...] = jnp.sum(self.wg_col[...], axis=0)
        self.weight_out = pltpu.make_async_copy(self.wg_out, self.weight_grad, self.out_sem.at[1])
        self.weight_out.start()

    def spread_step(self, h, piece, step):
        for way in range(2):
            if step == 4 and way != piece:
                continue
            tile = self.ga[h].at[self.ring((2 * way - 1) * step) * 2 + piece]
            self.landed(tile, self.d_sem.at[h, piece, way, step - 1])
            if step < 3 or (step == 3 and way == piece):
                self.send(tile, tile, self.d_send.at[0], self.d_sem.at[h, piece, way, step], self.ring_device(way))

    def grad_tile(self, h, piece, keep, step, core):
        reduce = self.along(1 - piece, step)
        x, y = (keep, reduce) if piece == 0 else (reduce, keep)
        return self.sums[h][self.table[LAST_B, ((x * SIDE + y) * 2 + core) * 2 + piece]]

    def grad_partner(self, h):
        for at, step in enumerate((*OTHERS, 0)):
            for piece in range(2):
                for keep in range(SIDE):
                    self.ps[h, at, piece, keep] = self.grad_tile(h, piece, keep, step, 1 - self.core).astype(BF16)
            self.send(self.ps.at[h, at], self.pr.at[h, at], self.e_send.at[h], self.p_sem.at[h, at], self.partner())

    def chip_tile(self, h, at, piece, keep):
        step = (*OTHERS, 0)[at]
        return self.grad_tile(h, piece, keep, step, self.core) + self.pr[h, at, piece, keep].astype(F32)

    def grad_first(self, h):
        for at, step in enumerate(OTHERS):
            self.landed(self.pr.at[h, at], self.p_sem.at[h, at])
            for piece in range(2):
                for keep in range(SIDE):
                    self.s1[h, piece, at, keep] = self.chip_tile(h, at, piece, keep).astype(BF16)
                self.send(
                    self.s1.at[h, piece, at], self.r1.at[h, piece, at], self.e_send.at[h],
                    self.r1_sem.at[h, piece], self.neighbour(1 - piece, step))

    def grad_second(self, h):
        self.landed(self.pr.at[h, 3], self.p_sem.at[h, 3])
        for piece in range(2):
            self.landed(self.r1.at[h, piece], self.r1_sem.at[h, piece])
            for keep in range(SIDE):
                value = self.chip_tile(h, 3, piece, keep)
                for at in range(3):
                    value = value + self.r1[h, piece, at, keep].astype(F32)
                self.axis_sum[h, piece, keep] = value
            for at, step in enumerate(OTHERS):
                self.s2[h, piece, at] = self.axis_sum[h, piece, self.along(piece, step)].astype(BF16)
                self.send(
                    self.s2.at[h, piece, at], self.r2.at[h, piece, at], self.e_send.at[h],
                    self.r2_sem.at[h, piece], self.neighbour(piece, step))

    def grad_end(self, h):
        for piece in range(2):
            self.landed(self.r2.at[h, piece], self.r2_sem.at[h, piece])
            value = self.axis_sum[h, piece, self.at[piece]]
            for at in range(3):
                value = value + self.r2[h, piece, at].astype(F32)
            self.fg_v[piece * T:(piece + 1) * T, h * T:(h + 1) * T] = value.T

    def finish(self):
        out = pltpu.make_async_copy(self.fg_v, self.feature_grad, self.out_sem.at[2])
        out.start()
        self.drain()
        self.landed(self.wg_row.at[pl.ds(0, 31)], self.w_sem.at[0])
        self.landed(self.wg_col.at[pl.ds(0, 7)], self.w_sem.at[2])
        self.hidden_out.wait()
        self.weight_out.wait()
        out.wait()

    def drain(self, stages="azde"):
        some = self.panel0
        if "a" in stages:
            for h in range(2):
                self.landed(some.at[pl.ds(0, 62)], self.a_send.at[h])
        if "z" in stages:
            self.landed(some.at[pl.ds(0, 28)], self.z_send.at[0])
        if "d" in stages:
            self.landed(some.at[pl.ds(0, 28)], self.d_send.at[0])
        if "e" in stages:
            for h in range(2):
                self.landed(some.at[pl.ds(0, 62)], self.e_send.at[h])

    def run(self):
        self.greet()
        self.load()
        self.met()
        self.gather_own(0)
        self.gather_own(1)
        self.index_table()
        self.gather_first(0)
        self.gather_first(1)
        self.gather_second(0)
        self.gather_partner(0)
        self.tiles_in.wait()
        self.forward(0)
        for piece in range(2):
            self.reduce_step(0, piece, 0)
        self.gather_second(1)
        for piece in range(2):
            self.reduce_step(0, piece, 1)
        self.gather_partner(1)
        self.forward(1)
        for piece in range(2):
            self.reduce_step(1, piece, 0)
        for piece in range(2):
            self.reduce_step(1, piece, 1)
            self.reduce_step(0, piece, 2)
        for piece in range(2):
            self.reduce_step(1, piece, 2)
            self.reduce_step(0, piece, 3)
        for piece in range(2):
            self.reduce_step(1, piece, 3)
            self.reduce_end(0, piece)
        self.reduce_end(1, 0)
        self.dense(0)
        self.reduce_end(1, 1)
        self.dense(1)
        self.weight_start()
        for step in (1, 2, 3):
            for piece in range(2):
                for h in range(2):
                    self.spread_step(h, piece, step)
        for piece in range(2):
            self.spread_step(0, piece, 4)
        self.backward(0)
        self.grad_partner(0)
        for piece in range(2):
            self.spread_step(1, piece, 4)
        self.grad_first(0)
        self.backward(1)
        self.grad_partner(1)
        self.grad_second(0)
        self.grad_first(1)
        self.weight_middle()
        self.grad_second(1)
        self.grad_end(0)
        self.weight_end()
        self.grad_end(1)
        self.finish()


def kernel(names, *refs):
    Layer(refs[:6], refs[6:9], dict(zip(names, refs[9:]))).run()


def hand_over(*refs):
    for source, target in zip(refs[:3], refs[3:]):
        target[...] = source[...]


def per_device(features, weight, tile_values, tile_coords, tile_count, cotangent):
    buffers = scratch()
    anywhere = pl.BlockSpec(memory_space=pl.ANY)
    shapes = (
        jax.ShapeDtypeStruct((256, 256), BF16),
        jax.ShapeDtypeStruct((8, 256), F32),
        jax.ShapeDtypeStruct((256, 256), F32),
    )
    results = pl.pallas_call(
        functools.partial(kernel, tuple(buffers)),
        out_shape=shapes,
        in_specs=[pl.BlockSpec(memory_space=pltpu.SMEM)] + [anywhere] * 5,
        out_specs=(anywhere, anywhere, anywhere),
        scratch_shapes=list(buffers.values()),
        compiler_params=pltpu.CompilerParams(
            collective_id=0, has_side_effects=True, vmem_limit_bytes=60 * 1024 * 1024),
        name="graph_layer",
    )(tile_count, features, weight, tile_values, tile_coords.T, cotangent)
    whole = pl.BlockSpec(memory_space=pltpu.VMEM)
    return pl.pallas_call(
        hand_over, out_shape=shapes, in_specs=[whole] * 3, out_specs=(whole, whole, whole), name="hand_over",
    )(*results)


def solution(mesh):
    return jax.shard_map(
        per_device,
        mesh=mesh,
        in_specs=(
            P(("row", "col"), None),
            P(),
            P(("row", "col"), None, None),
            P(("row", "col"), None),
            P(("row", "col")),
            P(("row", "col"), None),
        ),
        out_specs=(P(("row", "col"), None), P("row", None), P(("row", "col"), None)),
        check_vma=False,
    )
```

time: 570 us -> 87.4 us (0.15)
  waiting for transfers between devices: 431 us -> 0 us
  Pallas kernels: 0 us -> 86 us
  other arithmetic: 52.6 us -> 0 us
  local copies, waits for them, and re-layouts: 47.7 us -> 0 us
  matrix products: 22.9 us -> 0 us
  between operations: 14.6 us -> 1.29 us
    psum x1 -> x0, waiting for transfers between devices: 198 us -> none  [per_device(): total_weight = lax.psum(partial_weight, ('row', 'col'))]
    reduce_scatter x2 -> x0, waiting for transfers between devices: 141 us -> none  [the longest x1 102 us: per_device(): lax.psum_scatter(summed, 'row', scatter_dimension=0, tiled=True)]
    all_gather x2 -> x0, waiting for transfers between devices: 91.2 us -> none  [the longest x1 56.4 us: per_device(): panels = lax.all_gather(features, 'row', axis=0, tiled=True)]
    pallas_call x0 -> x2, Pallas kernels: none -> 86 us  [the longest x1 84.2 us: per_device(): pl.pallas_call(functools.partial(kernel, tuple(buffers)), out_shape=shape...]
    scatter-add x2 -> x0, other arithmetic: 51.8 us -> none  [tile_sums(): return empty.at[target].add(products, mode='drop')]
    dot_general x2 -> x0, local copies, waits for them, and re-layouts: 25.2 us -> none  [the longest x1 12.6 us: per_device(): jnp.einsum('kba,kbf->kaf', tile_values, chosen, preferred_element_type=jn...]
    dot_general x5 -> x0, matrix products: 22.9 us -> none  [the longest x1 9.1 us: per_device(): jnp.einsum('kab,kbf->kaf', tile_values, picked, preferred_element_type=jn...]
    gather x2 -> x0, local copies, waits for them, and re-layouts: 15.4 us -> none  [the longest x1 8.2 us: per_device(): picked = panels.reshape(col_tiles, tile_size, width)[col_ids]]
  transfers between devices with their start and end apart: 5 -> 0, of which waited for: 5 -> 0; matrix products, arithmetic and copies ran while one was open for 11% -> 0% of each run, Pallas kernels for 0% -> 0%
where the time goes in v2:
time: 87.4 us; the launch traced here: 87.2 us
  Pallas kernels  86 us (98%)
  between operations  1.29 us (1%)
    pallas_call x1, Pallas kernels, per_device(): pl.pallas_call(functools.partial(kernel, tuple(buffers)), out_shape=shape...  84.2 us
    pallas_call x1, Pallas kernels, per_device(): pl.pallas_call(hand_over, out_shape=shapes, in_specs=[whole] * 3, out_spe...  1.79 us

profile of v2, /device:TPU:1, one launch (start us, length us, event | category | flops | bytes accessed | tf_op | source)
XLA Modules:
  0.0 87.2 jit_solution(11665816448836895038)
XLA Ops:
  1.3 84.2 %graph_layer.1 = (bf16[256,256]{1,0:T(8,128)(2,1)}, f32[8,256]{1,0:T(8,128)}, f32[256,256]{1,0:T(8,128)}) custom-call(s32[1]{0:T(128)S(6)} %copy.9.refs_0_, bf16[256,256]{1,0:T(8,128)(2,1)} %refs_1_.1, bf16[256,256]{1,0:T(8,128)(2,1)} %refs_2_.1, bf16[96,128,128]{2,1,0:T(8,128)(2,1)} %refs_3_.1, s32[2,96]{1,0:T(2,128)} %bitcast.1, bf16[256,256]{1,0:T(8,128)(2,1)} %refs_5_.1), custom_call_target="tpu_custom_call" | custom-call | tf_op jit(solution)/shard_map/graph_layer/pallas_call | solution.py:480
  85.5 1.8 %hand_over.1 = (bf16[256,256]{1,0:T(8,128)(2,1)}, f32[8,256]{1,0:T(8,128)}, f32[256,256]{1,0:T(8,128)}) custom-call(bf16[256,256]{1,0:T(8,128)(2,1)} %get-tuple-element.6.refs_0_, f32[8,256]{1,0:T(8,128)} %get-tuple-element.7.refs_1_, f32[256,256]{1,0:T(8,128)} %get-tuple-element.8.refs_2_), custom_call_target="tpu_custom_call" | custom-call | tf_op jit(solution)/shard_map/hand_over/pallas_call | solution.py:491

commit v3 on v2

--- a/solution.py
+++ b/solution.py
@@ -24,6 +24,7 @@
 PREV_F, LAST_F, PREV_B, LAST_B, ROW_ID, PANEL_ID = range(6)
 
 OTHERS = (2, 1, -1)
+LINES = (2, 1, -1, 0)
 
 
 def gelu_pair(values):
@@ -50,7 +51,8 @@
         "sums0": pltpu.VMEM((SLOTS + 1, T, T), F32),
         "sums1": pltpu.VMEM((SLOTS + 1, T, T), F32),
         "zs": pltpu.VMEM((2, 2, 2, 4, T, T), BF16),
-        "zr": pltpu.VMEM((2, 2, 2, 4, T, T), BF16),
+        "zm": pltpu.VMEM((2, 2, 2, 2, T, T), BF16),
+        "zr": pltpu.VMEM((2, 2, 4, T, T), BF16),
         "agg": pltpu.VMEM((256, 256), BF16),
         "grad_pre": pltpu.VMEM((256, 256), BF16),
         "hid_v": pltpu.VMEM((256, 256), BF16),
@@ -61,11 +63,11 @@
         "wg_out": pltpu.VMEM((8, 256), F32),
         "ga0": pltpu.VMEM((ROW_TILES, T, T), BF16),
         "ga1": pltpu.VMEM((ROW_TILES, T, T), BF16),
-        "ps": pltpu.VMEM((2, 4, 2, SIDE, T, T), BF16),
-        "pr": pltpu.VMEM((2, 4, 2, SIDE, T, T), BF16),
-        "s1": pltpu.VMEM((2, 2, 3, SIDE, T, T), BF16),
-        "r1": pltpu.VMEM((2, 2, 3, SIDE, T, T), BF16),
-        "axis_sum": pltpu.VMEM((2, 2, SIDE, T, T), F32),
+        "ps": pltpu.VMEM((2, SIDE, 2, SIDE, T, T), BF16),
+        "pr": pltpu.VMEM((2, SIDE, 2, SIDE, T, T), BF16),
+        "s1": pltpu.VMEM((2, 2, SIDE, 3, T, T), BF16),
+        "r1": pltpu.VMEM((2, 2, SIDE, 3, T, T), BF16),
+        "axis_sum": pltpu.VMEM((2, 2, T, T), F32),
         "s2": pltpu.VMEM((2, 2, 3, T, T), BF16),
         "r2": pltpu.VMEM((2, 2, 3, T, T), BF16),
         "fg_v": pltpu.VMEM((256, 256), F32),
@@ -77,12 +79,14 @@
         "a2_sem": dma((2, 2, 4)),
         "ap_sem": dma((2,)),
         "z_send": dma((1,)),
-        "z_sem": dma((2, 2, 2, 4)),
+        "zm_sem": dma((2, 2, 2)),
+        "zr_sem": dma((2, 2)),
         "d_send": dma((1,)),
-        "d_sem": dma((2, 2, 2, 4)),
+        "dm_sem": dma((2, 2, 2)),
+        "dr_sem": dma((2, 2)),
         "e_send": dma((2,)),
         "p_sem": dma((2, 4)),
-        "r1_sem": dma((2, 2)),
+        "r1_sem": dma((2, 2, SIDE)),
         "r2_sem": dma((2, 2)),
         "w_sem": dma((4,)),
     }
@@ -115,8 +119,8 @@
     def ring(self, step):
         return lax.rem(self.z + step % RING, RING)
 
-    def ring_device(self, way):
-        return (self.row, self.ring(1 - 2 * way))
+    def ring_device(self, step):
+        return (self.row, self.ring(step))
 
     def panel_at(self, piece, first, second, core):
         return ((piece * 2 + core) * SIDE + first) * SIDE + second
@@ -155,10 +159,10 @@
 
     def friends(self):
         around = [self.neighbour(axis, step) for axis in range(2) for step in OTHERS]
-        return [self.partner(), self.ring_device(0), self.ring_device(1)] + around
+        return [self.partner()] + [self.ring_device(step) for step in (1, -1, 2, -2)] + around
 
     def met(self):
-        pl.semaphore_wait(pltpu.get_barrier_semaphore(), 9)
+        pl.semaphore_wait(pltpu.get_barrier_semaphore(), 11)
 
     def index_table(self):
         self.coords_in.wait()
@@ -245,26 +249,43 @@
 
         lax.fori_loop(0, SLOTS // UNROLL, block, 0)
 
-    def reduce_step(self, h, piece, step):
+    def row_sum(self, h, piece, step):
+        return self.sums[h][self.table[LAST_F, self.ring(step) * 2 + piece]]
+
+    def reduce_first(self, h, piece):
         for way in range(2):
-            if step == 0 and way != piece:
-                continue
             sign = 1 - 2 * way
-            block = self.ring(sign * (4 - step))
-            value = self.sums[h][self.table[LAST_F, block * 2 + piece]]
-            if step > 1 or (step == 1 and way == piece):
-                self.landed(self.zr.at[h, piece, way, step - 1], self.z_sem.at[h, piece, way, step - 1])
-                value = value + self.zr[h, piece, way, step - 1].astype(F32)
-            self.zs[h, piece, way, step] = value.astype(BF16)
-            self.send(
-                self.zs.at[h, piece, way, step], self.zr.at[h, piece, way, step], self.z_send.at[0],
-                self.z_sem.at[h, piece, way, step], self.ring_device(way))
+            stage, middle = self.zs.at[h, piece, way], self.zm.at[h, piece, way]
+            if way == piece:
+                stage[1] = self.row_sum(h, piece, 4 * sign).astype(BF16)
+                self.send(stage.at[1], middle.at[1], self.z_send.at[0], self.zm_sem.at[h, piece, way], self.ring_device(2 * sign))
+            stage[0] = self.row_sum(h, piece, 3 * sign).astype(BF16)
+            self.send(stage.at[0], middle.at[0], self.z_send.at[0], self.zm_sem.at[h, piece, way], self.ring_device(sign))
+        for way in range(2):
+            sign = 1 - 2 * way
+            stage = self.zs.at[h, piece, way]
+            stage[2] = self.row_sum(h, piece, sign).astype(BF16)
+            self.send(stage.at[2], self.zr.at[h, piece, way], self.z_send.at[0], self.zr_sem.at[h, piece], self.ring_device(sign))
+
+    def reduce_second(self, h, piece):
+        for way in range(2):
+            sign = 1 - 2 * way
+            stage, middle = self.zs.at[h, piece, way], self.zm.at[h, piece, way]
+            value = self.row_sum(h, piece, 2 * sign)
+            if way == piece:
+                self.landed(middle, self.zm_sem.at[h, piece, way])
+                value = value + middle[0].astype(F32) + middle[1].astype(F32)
+            else:
+                self.landed(middle.at[0], self.zm_sem.at[h, piece, way])
+                value = value + middle[0].astype(F32)
+            stage[3] = value.astype(BF16)
+            self.send(stage.at[3], self.zr.at[h, piece, 2 + way], self.z_send.at[0], self.zr_sem.at[h, piece], self.ring_device(2 * sign))
 
     def reduce_end(self, h, piece):
-        value = self.sums[h][self.table[LAST_F, self.z * 2 + piece]]
-        for way in range(2):
-            self.landed(self.zr.at[h, piece, way, 3], self.z_sem.at[h, piece, way, 3])
-            value = value + self.zr[h, piece, way, 3].astype(F32)
+        self.landed(self.zr.at[h, piece], self.zr_sem.at[h, piece])
+        value = self.row_sum(h, piece, 0)
+        for came in range(4):
+            value = value + self.zr[h, piece, came].astype(F32)
         self.agg[piece * T:(piece + 1) * T, h * T:(h + 1) * T] = value.astype(BF16)
 
     def dense(self, piece):
@@ -281,10 +302,7 @@
             self.ga[h][self.z * 2 + piece] = turned[h * T:(h + 1) * T]
         self.hid_v[rows, :] = result.astype(BF16)
         self.grad_pre[rows, :] = grad_pre
-        for h in range(2):
-            mine = self.ga[h].at[self.z * 2 + piece]
-            for way in range(2):
-                self.send(mine, mine, self.d_send.at[0], self.d_sem.at[h, piece, way, 0], self.ring_device(way))
+        self.spread_own(0, piece)
 
     def weight_start(self):
         self.hidden_out = pltpu.make_async_copy(self.hid_v, self.hidden, self.out_sem.at[0])
@@ -320,60 +338,72 @@
         self.weight_out = pltpu.make_async_copy(self.wg_out, self.weight_grad, self.out_sem.at[1])
         self.weight_out.start()
 
-    def spread_step(self, h, piece, step):
+    def spread(self, h, piece, source, step, sem):
+        tile = self.ga[h].at[self.ring(source) * 2 + piece]
+        self.send(tile, tile, self.d_send.at[0], sem, self.ring_device(step))
+
+    def spread_own(self, h, piece):
         for way in range(2):
-            if step == 4 and way != piece:
-                continue
-            tile = self.ga[h].at[self.ring((2 * way - 1) * step) * 2 + piece]
-            self.landed(tile, self.d_sem.at[h, piece, way, step - 1])
-            if step < 3 or (step == 3 and way == piece):
-                self.send(tile, tile, self.d_send.at[0], self.d_sem.at[h, piece, way, step], self.ring_device(way))
+            self.spread(h, piece, 0, 2 - 4 * way, self.dm_sem.at[h, piece, way])
+        for way in range(2):
+            self.spread(h, piece, 0, 1 - 2 * way, self.dr_sem.at[h, piece])
+
+    def spread_on(self, h, piece):
+        for way in range(2):
+            sign = 1 - 2 * way
+            tile = self.ga[h].at[self.ring(-2 * sign) * 2 + piece]
+            self.landed(tile, self.dm_sem.at[h, piece, way])
+            if way == piece:
+                self.spread(h, piece, -2 * sign, 2 * sign, self.dr_sem.at[h, piece])
+            self.spread(h, piece, -2 * sign, sign, self.dr_sem.at[h, piece])
+
+    def spread_end(self, h):
+        for piece in range(2):
+            self.landed(self.ga[h].at[pl.ds(0, 5)], self.dr_sem.at[h, piece])
 
     def grad_tile(self, h, piece, keep, step, core):
         reduce = self.along(1 - piece, step)
         x, y = (keep, reduce) if piece == 0 else (reduce, keep)
         return self.sums[h][self.table[LAST_B, ((x * SIDE + y) * 2 + core) * 2 + piece]]
 
-    def grad_partner(self, h):
-        for at, step in enumerate((*OTHERS, 0)):
+    def grad_partner(self, h, line):
+        keep = {piece: self.along(piece, LINES[line]) for piece in range(2)}
+        for piece in range(2):
+            for at, step in enumerate(LINES):
+                self.ps[h, line, piece, at] = self.grad_tile(h, piece, keep[piece], step, 1 - self.core).astype(BF16)
+        self.send(self.ps.at[h, line], self.pr.at[h, line], self.e_send.at[h], self.p_sem.at[h, line], self.partner())
+
+    def chip_tile(self, h, line, piece, at):
+        keep = self.along(piece, LINES[line])
+        return self.grad_tile(h, piece, keep, LINES[at], self.core) + self.pr[h, line, piece, at].astype(F32)
+
+    def grad_first(self, h, line):
+        self.landed(self.pr.at[h, line], self.p_sem.at[h, line])
+        for at, step in enumerate(OTHERS):
             for piece in range(2):
-                for keep in range(SIDE):
-                    self.ps[h, at, piece, keep] = self.grad_tile(h, piece, keep, step, 1 - self.core).astype(BF16)
-            self.send(self.ps.at[h, at], self.pr.at[h, at], self.e_send.at[h], self.p_sem.at[h, at], self.partner())
-
-    def chip_tile(self, h, at, piece, keep):
-        step = (*OTHERS, 0)[at]
-        return self.grad_tile(h, piece, keep, step, self.core) + self.pr[h, at, piece, keep].astype(F32)
-
-    def grad_first(self, h):
-        for at, step in enumerate(OTHERS):
-            self.landed(self.pr.at[h, at], self.p_sem.at[h, at])
-            for piece in range(2):
-                for keep in range(SIDE):
-                    self.s1[h, piece, at, keep] = self.chip_tile(h, at, piece, keep).astype(BF16)
+                self.s1[h, piece, line, at] = self.chip_tile(h, line, piece, at).astype(BF16)
                 self.send(
-                    self.s1.at[h, piece, at], self.r1.at[h, piece, at], self.e_send.at[h],
-                    self.r1_sem.at[h, piece], self.neighbour(1 - piece, step))
-
-    def grad_second(self, h):
-        self.landed(self.pr.at[h, 3], self.p_sem.at[h, 3])
-        for piece in range(2):
-            self.landed(self.r1.at[h, piece], self.r1_sem.at[h, piece])
-            for keep in range(SIDE):
-                value = self.chip_tile(h, 3, piece, keep)
-                for at in range(3):
-                    value = value + self.r1[h, piece, at, keep].astype(F32)
-                self.axis_sum[h, piece, keep] = value
-            for at, step in enumerate(OTHERS):
-                self.s2[h, piece, at] = self.axis_sum[h, piece, self.along(piece, step)].astype(BF16)
-                self.send(
-                    self.s2.at[h, piece, at], self.r2.at[h, piece, at], self.e_send.at[h],
-                    self.r2_sem.at[h, piece], self.neighbour(piece, step))
+                    self.s1.at[h, piece, line, at], self.r1.at[h, piece, line, at], self.e_send.at[h],
+                    self.r1_sem.at[h, piece, line], self.neighbour(1 - piece, step))
+
+    def grad_second(self, h, line):
+        for piece in range(2):
+            self.landed(self.r1.at[h, piece, line], self.r1_sem.at[h, piece, line])
+            value = self.chip_tile(h, line, piece, 3)
+            for at in range(3):
+                value = value + self.r1[h, piece, line, at].astype(F32)
+            if line == 3:
+                self.axis_sum[h, piece] = value
+                continue
+            self.s2[h, piece, line] = value.astype(BF16)
+            self.send(
+                self.s2.at[h, piece, line], self.r2.at[h, piece, line], self.e_send.at[h],
+                self.r2_sem.at[h, piece], self.neighbour(piece, LINES[line]))
 
     def grad_end(self, h):
         for piece in range(2):
             self.landed(self.r2.at[h, piece], self.r2_sem.at[h, piece])
-            value = self.axis_sum[h, piece, self.at[piece]]
+            value = self.axis_sum[h, piece]
             for at in range(3):
                 value = value + self.r2[h, piece, at].astype(F32)
             self.fg_v[piece * T:(piece + 1) * T, h * T:(h + 1) * T] = value.T
@@ -415,45 +445,43 @@
         self.tiles_in.wait()
         self.forward(0)
         for piece in range(2):
-            self.reduce_step(0, piece, 0)
+            self.reduce_first(0, piece)
         self.gather_second(1)
         for piece in range(2):
-            self.reduce_step(0, piece, 1)
+            self.reduce_second(0, piece)
         self.gather_partner(1)
         self.forward(1)
         for piece in range(2):
-            self.reduce_step(1, piece, 0)
-        for piece in range(2):
-            self.reduce_step(1, piece, 1)
-            self.reduce_step(0, piece, 2)
-        for piece in range(2):
-            self.reduce_step(1, piece, 2)
-            self.reduce_step(0, piece, 3)
-        for piece in range(2):
-            self.reduce_step(1, piece, 3)
+            self.reduce_first(1, piece)
+        for piece in range(2):
             self.reduce_end(0, piece)
-        self.reduce_end(1, 0)
-        self.dense(0)
-        self.reduce_end(1, 1)
-        self.dense(1)
+        for piece in range(2):
+            self.reduce_second(1, piece)
+        for piece in range(2):
+            self.reduce_end(1, piece)
+            self.dense(piece)
+        for piece in range(2):
+            self.spread_own(1, piece)
         self.weight_start()
-        for step in (1, 2, 3):
+        for h in range(2):
             for piece in range(2):
-                for h in range(2):
-                    self.spread_step(h, piece, step)
-        for piece in range(2):
-            self.spread_step(0, piece, 4)
+                self.spread_on(h, piece)
+        self.spread_end(0)
         self.backward(0)
-        self.grad_partner(0)
-        for piece in range(2):
-            self.spread_step(1, piece, 4)
-        self.grad_first(0)
+        for line in range(4):
+            self.grad_partner(0, line)
+        for line in range(4):
+            self.grad_first(0, line)
+        self.spread_end(1)
         self.backward(1)
-        self.grad_partner(1)
-        self.grad_second(0)
-        self.grad_first(1)
+        for line in range(4):
+            self.grad_partner(1, line)
+        for line in range(4):
+            self.grad_second(0, line)
+            self.grad_first(1, line)
         self.weight_middle()
-        self.grad_second(1)
+        for line in range(4):
+            self.grad_second(1, line)
         self.grad_end(0)
         self.weight_end()
         self.grad_end(1)

time: 87.4 us -> 81.2 us (0.929)
  Pallas kernels: 86 us -> 79.8 us
    pallas_call x1, Pallas kernels: 84.2 us -> 78 us  [per_device(): pl.pallas_call(functools.partial(kernel, tuple(buffers)), out_shape=shape...]
where the time goes in v3:
time: 81.2 us; the launch traced here: 81.1 us
  Pallas kernels  79.8 us (98%)
  between operations  1.29 us (2%)
    pallas_call x1, Pallas kernels, per_device(): pl.pallas_call(functools.partial(kernel, tuple(buffers)), out_shape=shape...  78 us
    pallas_call x1, Pallas kernels, per_device(): pl.pallas_call(hand_over, out_shape=shapes, in_specs=[whole] * 3, out_spe...  1.79 us

profile of v3, /device:TPU:1, one launch (start us, length us, event | category | flops | bytes accessed | tf_op | source)
XLA Modules:
  0.0 81.1 jit_solution(5771001666463643292)
XLA Ops:
  1.3 78.0 %graph_layer.1 = (bf16[256,256]{1,0:T(8,128)(2,1)}, f32[8,256]{1,0:T(8,128)}, f32[256,256]{1,0:T(8,128)}) custom-call(s32[1]{0:T(128)S(6)} %copy.9.refs_0_, bf16[256,256]{1,0:T(8,128)(2,1)} %refs_1_.1, bf16[256,256]{1,0:T(8,128)(2,1)} %refs_2_.1, bf16[96,128,128]{2,1,0:T(8,128)(2,1)} %refs_3_.1, s32[2,96]{1,0:T(2,128)} %bitcast.1, bf16[256,256]{1,0:T(8,128)(2,1)} %refs_5_.1), custom_call_target="tpu_custom_call" | custom-call | tf_op jit(solution)/shard_map/graph_layer/pallas_call | solution.py:508
  79.3 1.8 %hand_over.1 = (bf16[256,256]{1,0:T(8,128)(2,1)}, f32[8,256]{1,0:T(8,128)}, f32[256,256]{1,0:T(8,128)}) custom-call(bf16[256,256]{1,0:T(8,128)(2,1)} %get-tuple-element.6.refs_0_, f32[8,256]{1,0:T(8,128)} %get-tuple-element.7.refs_1_, f32[256,256]{1,0:T(8,128)} %get-tuple-element.8.refs_2_), custom_call_target="tpu_custom_call" | custom-call | tf_op jit(solution)/shard_map/hand_over/pallas_call | solution.py:519

commit v4 on v3

--- a/solution.py
+++ b/solution.py
@@ -19,7 +19,7 @@
 SLOTS = 96
 ROW_TILES = 16
 COL_TILES = 64
-UNROLL = 16
+UNROLL = 32
 
 PREV_F, LAST_F, PREV_B, LAST_B, ROW_ID, PANEL_ID = range(6)
 
@@ -44,6 +44,7 @@
         "weight_v": pltpu.VMEM((256, 256), BF16),
         "cot_v": pltpu.VMEM((256, 256), BF16),
         "coords_v": pltpu.VMEM((2, SLOTS), jnp.int32),
+        "count_s": pltpu.SMEM((1,), jnp.int32),
         "table_v": pltpu.VMEM((8, SLOTS), jnp.int32),
         "table": pltpu.SMEM((8, SLOTS), jnp.int32),
         "panel0": pltpu.VMEM((COL_TILES, T, T), BF16),
@@ -72,7 +73,7 @@
         "r2": pltpu.VMEM((2, 2, 3, T, T), BF16),
         "fg_v": pltpu.VMEM((256, 256), F32),
         "own_sem": dma((2,)),
-        "in_sem": dma((5,)),
+        "in_sem": dma((6,)),
         "out_sem": dma((3,)),
         "a_send": dma((2,)),
         "a1_sem": dma((2, 2, 3)),
@@ -144,12 +145,13 @@
                 copy.start()
         sem = self.in_sem
         self.coords_in = pltpu.make_async_copy(self.coords, self.coords_v, sem.at[0])
+        self.count_in = pltpu.make_async_copy(self.count, self.count_s, sem.at[5])
         self.tiles_in = pltpu.make_async_copy(self.tile_values, self.tiles, sem.at[1])
         self.dense_in = (
             pltpu.make_async_copy(self.weight, self.weight_v, sem.at[2]),
             pltpu.make_async_copy(self.cotangent, self.cot_v, sem.at[3]),
         )
-        for copy in (self.coords_in, self.tiles_in, *self.dense_in):
+        for copy in (self.coords_in, self.count_in, self.tiles_in, *self.dense_in):
             copy.start()
 
     def greet(self):
@@ -166,9 +168,10 @@
 
     def index_table(self):
         self.coords_in.wait()
+        self.count_in.wait()
         slot = lax.broadcasted_iota(jnp.int32, (SLOTS, SLOTS), 0)
         lane = lax.broadcasted_iota(jnp.int32, (SLOTS, SLOTS), 1)
-        live = slot < self.count[0]
+        live = slot < self.count_s[0]
         lines = [None] * 8
         for column, prev, last in ((0, PREV_F, LAST_F), (1, PREV_B, LAST_B)):
             across = self.coords_v[column:column + 1, :]
@@ -204,8 +207,6 @@
             tile = self.panel[h].at[at]
             for step in OTHERS:
                 self.send(tile, tile, self.a_send.at[h], self.a1_sem.at[h, piece, step % SIDE - 1], self.neighbour(piece, step))
-        for piece in range(2):
-            self.gather_across(h, piece, 0)
 
     def gather_first(self, h):
         for step in (1, -1, 2):
@@ -261,6 +262,8 @@
                 self.send(stage.at[1], middle.at[1], self.z_send.at[0], self.zm_sem.at[h, piece, way], self.ring_device(2 * sign))
             stage[0] = self.row_sum(h, piece, 3 * sign).astype(BF16)
             self.send(stage.at[0], middle.at[0], self.z_send.at[0], self.zm_sem.at[h, piece, way], self.ring_device(sign))
+
+    def reduce_near(self, h, piece):
         for way in range(2):
             sign = 1 - 2 * way
             stage = self.zs.at[h, piece, way]
@@ -436,9 +439,13 @@
         self.load()
         self.met()
         self.gather_own(0)
+        for piece in range(2):
+            self.gather_across(0, piece, 0)
         self.gather_own(1)
         self.index_table()
         self.gather_first(0)
+        for piece in range(2):
+            self.gather_across(1, piece, 0)
         self.gather_first(1)
         self.gather_second(0)
         self.gather_partner(0)
@@ -446,6 +453,8 @@
         self.forward(0)
         for piece in range(2):
             self.reduce_first(0, piece)
+        for piece in range(2):
+            self.reduce_near(0, piece)
         self.gather_second(1)
         for piece in range(2):
             self.reduce_second(0, piece)
@@ -454,6 +463,8 @@
         for piece in range(2):
             self.reduce_first(1, piece)
         for piece in range(2):
+            self.reduce_near(1, piece)
+        for piece in range(2):
             self.reduce_end(0, piece)
         for piece in range(2):
             self.reduce_second(1, piece)
@@ -461,11 +472,12 @@
             self.reduce_end(1, piece)
             self.dense(piece)
         for piece in range(2):
+            self.spread_on(0, piece)
+        for piece in range(2):
             self.spread_own(1, piece)
         self.weight_start()
-        for h in range(2):
-            for piece in range(2):
-                self.spread_on(h, piece)
+        for piece in range(2):
+            self.spread_on(1, piece)
         self.spread_end(0)
         self.backward(0)
         for line in range(4):
@@ -508,7 +520,7 @@
     results = pl.pallas_call(
         functools.partial(kernel, tuple(buffers)),
         out_shape=shapes,
-        in_specs=[pl.BlockSpec(memory_space=pltpu.SMEM)] + [anywhere] * 5,
+        in_specs=[anywhere] * 6,
         out_specs=(anywhere, anywhere, anywhere),
         scratch_shapes=list(buffers.values()),
         compiler_params=pltpu.CompilerParams(

time: 81.2 us -> 78.6 us (0.968)
  Pallas kernels: 79.8 us -> 77.2 us
    pallas_call x1, Pallas kernels: 78 us -> 75.4 us  [per_device(): pl.pallas_call(functools.partial(kernel, tuple(buffers)), out_shape=shape...]
where the time goes in v4:
time: 78.6 us; the launch traced here: 78.5 us
  Pallas kernels  77.2 us (98%)
  between operations  1.29 us (2%)
    pallas_call x1, Pallas kernels, per_device(): pl.pallas_call(functools.partial(kernel, tuple(buffers)), out_shape=shape...  75.4 us
    pallas_call x1, Pallas kernels, per_device(): pl.pallas_call(hand_over, out_shape=shapes, in_specs=[whole] * 3, out_spe...  1.79 us

profile of v4, /device:TPU:1, one launch (start us, length us, event | category | flops | bytes accessed | tf_op | source)
XLA Modules:
  0.0 78.5 jit_solution(3128607608863682638)
XLA Ops:
  1.3 75.4 %graph_layer.1 = (bf16[256,256]{1,0:T(8,128)(2,1)}, f32[8,256]{1,0:T(8,128)}, f32[256,256]{1,0:T(8,128)}) custom-call(s32[1]{0:T(128)S(6)} %copy.9.refs_0_, bf16[256,256]{1,0:T(8,128)(2,1)} %refs_1_.1, bf16[256,256]{1,0:T(8,128)(2,1)} %refs_2_.1, bf16[96,128,128]{2,1,0:T(8,128)(2,1)} %refs_3_.1, s32[2,96]{1,0:T(2,128)} %bitcast.1, bf16[256,256]{1,0:T(8,128)(2,1)} %refs_5_.1), custom_call_target="tpu_custom_call" | custom-call | tf_op jit(solution)/shard_map/graph_layer/pallas_call | solution.py:520
  76.7 1.8 %hand_over.1 = (bf16[256,256]{1,0:T(8,128)(2,1)}, f32[8,256]{1,0:T(8,128)}, f32[256,256]{1,0:T(8,128)}) custom-call(bf16[256,256]{1,0:T(8,128)(2,1)} %get-tuple-element.6.refs_0_, f32[8,256]{1,0:T(8,128)} %get-tuple-element.7.refs_1_, f32[256,256]{1,0:T(8,128)} %get-tuple-element.8.refs_2_), custom_call_target="tpu_custom_call" | custom-call | tf_op jit(solution)/shard_map/hand_over/pallas_call | solution.py:531

commit v5 on v4

--- a/solution.py
+++ b/solution.py
@@ -68,16 +68,18 @@
         "pr": pltpu.VMEM((2, SIDE, 2, SIDE, T, T), BF16),
         "s1": pltpu.VMEM((2, 2, SIDE, 3, T, T), BF16),
         "r1": pltpu.VMEM((2, 2, SIDE, 3, T, T), BF16),
+        "rf": pltpu.VMEM((2, 2, 2, T, T), BF16),
         "axis_sum": pltpu.VMEM((2, 2, T, T), F32),
         "s2": pltpu.VMEM((2, 2, 3, T, T), BF16),
-        "r2": pltpu.VMEM((2, 2, 3, T, T), BF16),
+        "r2": pltpu.VMEM((2, 2, 4, T, T), BF16),
         "fg_v": pltpu.VMEM((256, 256), F32),
         "own_sem": dma((2,)),
         "in_sem": dma((6,)),
-        "out_sem": dma((3,)),
+        "out_sem": dma((4,)),
         "a_send": dma((2,)),
         "a1_sem": dma((2, 2, 3)),
         "a2_sem": dma((2, 2, 4)),
+        "a3_sem": dma((2, 2)),
         "ap_sem": dma((2,)),
         "z_send": dma((1,)),
         "zm_sem": dma((2, 2, 2)),
@@ -88,6 +90,7 @@
         "e_send": dma((2,)),
         "p_sem": dma((2, 4)),
         "r1_sem": dma((2, 2, SIDE)),
+        "rf_sem": dma((2, 2)),
         "r2_sem": dma((2, 2)),
         "w_sem": dma((4,)),
     }
@@ -136,7 +139,7 @@
         pltpu.make_async_copy(ref, ref, sem).wait()
 
     def load(self):
-        self.own = []
+        self.grads_out = []
         for h in range(2):
             for piece in range(2):
                 at = self.panel_at(piece, self.at[piece], self.at[1 - piece], self.core)
@@ -195,10 +198,20 @@
 
     def gather_across(self, h, piece, step1):
         first = self.along(piece, step1)
-        at = self.panel_at(piece, first, self.at[1 - piece], self.core)
-        tile = self.panel[h].at[at]
+        tile = self.panel[h].at[self.panel_at(piece, first, self.at[1 - piece], self.core)]
         for step in OTHERS:
-            self.send(tile, tile, self.a_send.at[h], self.a2_sem.at[h, piece, step1 % SIDE], self.neighbour(1 - piece, step))
+            if step == 2 and step1 in (1, -1):
+                continue
+            sem = self.a3_sem.at[h, piece] if step == 2 and step1 == 0 else self.a2_sem.at[h, piece, step1 % SIDE]
+            self.send(tile, tile, self.a_send.at[h], sem, self.neighbour(1 - piece, step))
+
+    def gather_far(self, h):
+        for piece in range(2):
+            at = self.panel_at(piece, self.at[piece], self.along(1 - piece, 2), self.core)
+            tile = self.panel[h].at[at]
+            self.landed(tile, self.a3_sem.at[h, piece])
+            for step in (1, -1):
+                self.send(tile, tile, self.a_send.at[h], self.a2_sem.at[h, piece, -step % SIDE], self.neighbour(piece, step))
 
     def gather_own(self, h):
         self.landed(self.panel[h].at[pl.ds(0, 2)], self.own_sem.at[h])
@@ -219,7 +232,7 @@
         for step1 in (0, -1, 1, 2):
             for piece in range(2):
                 first = self.panel_at(piece, self.along(piece, step1), 0, self.core)
-                self.landed(self.panel[h].at[pl.ds(first, 3)], self.a2_sem.at[h, piece, step1 % SIDE])
+                self.landed(self.panel[h].at[pl.ds(first, 2 if step1 == 0 else 3)], self.a2_sem.at[h, piece, step1 % SIDE])
                 line = self.panel[h].at[pl.ds(first, SIDE)]
                 self.send(line, line, self.a_send.at[h], self.ap_sem.at[h], self.partner())
 
@@ -383,17 +396,32 @@
     def grad_first(self, h, line):
         self.landed(self.pr.at[h, line], self.p_sem.at[h, line])
         for at, step in enumerate(OTHERS):
+            if at == 0 and line == 3:
+                continue
             for piece in range(2):
                 self.s1[h, piece, line, at] = self.chip_tile(h, line, piece, at).astype(BF16)
-                self.send(
-                    self.s1.at[h, piece, line, at], self.r1.at[h, piece, line, at], self.e_send.at[h],
-                    self.r1_sem.at[h, piece, line], self.neighbour(1 - piece, step))
+                if at == 0 and line in (1, 2):
+                    target, sem, device = self.rf.at[h, piece, line - 1], self.rf_sem.at[h, piece], self.neighbour(piece, LINES[line])
+                else:
+                    target, sem = self.r1.at[h, piece, line, at], self.r1_sem.at[h, piece, line]
+                    device = self.neighbour(1 - piece, step)
+                self.send(self.s1.at[h, piece, line, at], target, self.e_send.at[h], sem, device)
+
+    def grad_far(self, h):
+        for piece in range(2):
+            self.landed(self.rf.at[h, piece], self.rf_sem.at[h, piece])
+            value = self.chip_tile(h, 3, piece, 0) + self.rf[h, piece, 0].astype(F32) + self.rf[h, piece, 1].astype(F32)
+            self.s1[h, piece, 3, 0] = value.astype(BF16)
+            self.send(
+                self.s1.at[h, piece, 3, 0], self.r2.at[h, piece, 3], self.e_send.at[h],
+                self.r2_sem.at[h, piece], self.neighbour(1 - piece, 2))
 
     def grad_second(self, h, line):
-        for piece in range(2):
-            self.landed(self.r1.at[h, piece, line], self.r1_sem.at[h, piece, line])
+        far = 0 if line == 0 else 1
+        for piece in range(2):
+            self.landed(self.r1.at[h, piece, line, pl.ds(far, 3 - far)], self.r1_sem.at[h, piece, line])
             value = self.chip_tile(h, line, piece, 3)
-            for at in range(3):
+            for at in range(far, 3):
                 value = value + self.r1[h, piece, line, at].astype(F32)
             if line == 3:
                 self.axis_sum[h, piece] = value
@@ -407,19 +435,22 @@
         for piece in range(2):
             self.landed(self.r2.at[h, piece], self.r2_sem.at[h, piece])
             value = self.axis_sum[h, piece]
-            for at in range(3):
+            for at in range(4):
                 value = value + self.r2[h, piece, at].astype(F32)
             self.fg_v[piece * T:(piece + 1) * T, h * T:(h + 1) * T] = value.T
+        columns = pl.ds(h * T, T)
+        out = pltpu.make_async_copy(self.fg_v.at[:, columns], self.feature_grad.at[:, columns], self.out_sem.at[2 + h])
+        out.start()
+        self.grads_out.append(out)
 
     def finish(self):
-        out = pltpu.make_async_copy(self.fg_v, self.feature_grad, self.out_sem.at[2])
-        out.start()
         self.drain()
         self.landed(self.wg_row.at[pl.ds(0, 31)], self.w_sem.at[0])
         self.landed(self.wg_col.at[pl.ds(0, 7)], self.w_sem.at[2])
         self.hidden_out.wait()
         self.weight_out.wait()
-        out.wait()
+        for out in self.grads_out:
+            out.wait()
 
     def drain(self, stages="azde"):
         some = self.panel0
@@ -444,9 +475,11 @@
         self.gather_own(1)
         self.index_table()
         self.gather_first(0)
+        self.gather_far(0)
         for piece in range(2):
             self.gather_across(1, piece, 0)
         self.gather_first(1)
+        self.gather_far(1)
         self.gather_second(0)
         self.gather_partner(0)
         self.tiles_in.wait()
@@ -490,10 +523,14 @@
             self.grad_partner(1, line)
         for line in range(4):
             self.grad_second(0, line)
+            if line == 2:
+                self.grad_far(0)
             self.grad_first(1, line)
         self.weight_middle()
         for line in range(4):
             self.grad_second(1, line)
+            if line == 2:
+                self.grad_far(1)
         self.grad_end(0)
         self.weight_end()
         self.grad_end(1)
@@ -505,8 +542,16 @@
 
 
 def hand_over(*refs):
-    for source, target in zip(refs[:3], refs[3:]):
-        target[...] = source[...]
+    sources, targets, middle, sem = refs[:3], refs[3:6], refs[6:9], refs[9]
+    inward = [pltpu.make_async_copy(a, b, sem.at[i]) for i, (a, b) in enumerate(zip(sources, middle))]
+    outward = [pltpu.make_async_copy(a, b, sem.at[3 + i]) for i, (a, b) in enumerate(zip(middle, targets))]
+    for copy in inward:
+        copy.start()
+    for came, leaves in zip(inward, outward):
+        came.wait()
+        leaves.start()
+    for copy in outward:
+        copy.wait()
 
 
 def per_device(features, weight, tile_values, tile_coords, tile_count, cotangent):
@@ -527,9 +572,10 @@
             collective_id=0, has_side_effects=True, vmem_limit_bytes=60 * 1024 * 1024),
         name="graph_layer",
     )(tile_count, features, weight, tile_values, tile_coords.T, cotangent)
-    whole = pl.BlockSpec(memory_space=pltpu.VMEM)
     return pl.pallas_call(
-        hand_over, out_shape=shapes, in_specs=[whole] * 3, out_specs=(whole, whole, whole), name="hand_over",
+        hand_over, out_shape=shapes, in_specs=[anywhere] * 3, out_specs=(anywhere, anywhere, anywhere),
+        scratch_shapes=[pltpu.VMEM(one.shape, one.dtype) for one in shapes] + [pltpu.SemaphoreType.DMA((6,))],
+        name="hand_over",
     )(*results)
 
 

time: 78.6 us -> 78.3 us (level)
  no operation moved by 1% of the time
where the time goes in v5:
time: 78.3 us; the launch traced here: 78.2 us
  Pallas kernels  76.9 us (98%)
  between operations  1.29 us (2%)
    pallas_call x1, Pallas kernels, per_device(): pl.pallas_call(functools.partial(kernel, tuple(buffers)), out_shape=shape...  75.1 us
    pallas_call x1, Pallas kernels, per_device(): pl.pallas_call(hand_over, out_shape=shapes, in_specs=[anywhere] * 3, out_...  1.79 us

profile of v5, /device:TPU:1, one launch (start us, length us, event | category | flops | bytes accessed | tf_op | source)
XLA Modules:
  0.0 78.2 jit_solution(17671155958608119454)
XLA Ops:
  1.3 75.1 %graph_layer.1 = (bf16[256,256]{1,0:T(8,128)(2,1)}, f32[8,256]{1,0:T(8,128)}, f32[256,256]{1,0:T(8,128)}) custom-call(s32[1]{0:T(128)S(6)} %copy.9.refs_0_, bf16[256,256]{1,0:T(8,128)(2,1)} %refs_1_.1, bf16[256,256]{1,0:T(8,128)(2,1)} %refs_2_.1, bf16[96,128,128]{2,1,0:T(8,128)(2,1)} %refs_3_.1, s32[2,96]{1,0:T(2,128)} %bitcast.1, bf16[256,256]{1,0:T(8,128)(2,1)} %refs_5_.1), custom_call_target="tpu_custom_call" | custom-call | tf_op jit(solution)/shard_map/graph_layer/pallas_call | solution.py:565
  76.4 1.8 %hand_over.1 = (bf16[256,256]{1,0:T(8,128)(2,1)}, f32[8,256]{1,0:T(8,128)}, f32[256,256]{1,0:T(8,128)}) custom-call(bf16[256,256]{1,0:T(8,128)(2,1)} %get-tuple-element.6.refs_0_, f32[8,256]{1,0:T(8,128)} %get-tuple-element.7.refs_1_, f32[256,256]{1,0:T(8,128)} %get-tuple-element.8.refs_2_), custom_call_target="tpu_custom_call" | custom-call | tf_op jit(solution)/shard_map/hand_over/pallas_call | solution.py:575
